TPU v7x, 128 devices: a whole 4x4x4 slice. The times are simulated.
128 devices in a mesh: row: 8 (over z, core), col: 16 (over x, y).
Axes of the slice: x: 4, y: 4, z: 4, core: 2. Of those that a mesh axis runs over, the one named last changes fastest.
Arguments:
- velocity: float32 [2, 512, 128, 384], P(None, 'col', 'row'), may hold values from -6 to 6
- synthesis: float32 [384, 384], replicated
- analysis: float32 [384, 384], replicated
- radial_eigen: float32 [384], replicated, may hold values from 0.05 to 4
- pair_list: int32 [256, 2], replicated, may hold values from 0 to 511, as said below
- owner_slot: int32 [256], replicated, may hold values from 0 to 255, each once
- freq_list: int32 [4], replicated, may hold values from 0 to 255
- snap_index: int32 [1], replicated, may hold values from 0 to 254
- block_dft: float32 [256, 4, 2, 384], P(('row', 'col')), may hold values from -6 to 6
- spectra: float32 [256, 4, 2, 384, 384], P(('row', 'col')), may hold values from -6 to 6
Outputs:
- velocity_next: float32 [2, 512, 128, 384], P(None, 'col', 'row')
- block_sums: float32 [256, 4, 2, 384], P(('row', 'col'))
- spectra_next: float32 [256, 4, 2, 384, 384], P(('row', 'col'))
Inputs may be any that keep to these rules, and one draw needn't show every extreme that they name: `pair_list`: the pairs are distinct; the axial index is below 128 and the wavenumber below 512. Of the devices of the solver layout (row index times the size of col plus col index, holding axial indices row * 16 onward and wavenumbers col * 512 / size of col onward), each holds at most 8 selected pairs and some hold exactly 8. `owner_slot`: each slot once.
All inputs are finite; a program needn't handle non-finite values.
Results may differ from a plain program's by a relative error of at most 0.0001.
Values sent between devices are 32-bit elements; how exact they have to be, the bound alone decides.
No kernel may reach another device: no remote copies, remote signals or barrier semaphores. Data moves between devices by JAX's collectives and lax.ppermute only.
A program may use at most 128 MiB of HBM per device.

v0:
```python
import math

import jax
import jax.numpy as jnp
from jax import lax
from jax.sharding import PartitionSpec as P

NBLK = 256
HOLD = 8


viscosity = 4e-06
axial_scale = 2.0
nonlinear_gain = 0.1
highest = lax.Precision.HIGHEST


def sent_together(arrays, axis, split_dim, concat_dim, along):
    both = jnp.concatenate(arrays, axis=along)
    whole, at, outs = (
        lax.all_to_all(both, axis, split_axis=split_dim, concat_axis=concat_dim, tiled=True),
        0,
        [],
    )
    for a in arrays:
        outs.append(lax.slice_in_dim(whole, at, at + a.shape[along], axis=along))
        at += a.shape[along]
    return tuple(outs)


def circle_tables(mode_count, point_count):
    mode_ids = jnp.arange(mode_count, dtype=jnp.int32)[:, None]
    point_ids = jnp.arange(point_count, dtype=jnp.int32)[None, :]
    angle = (mode_ids * point_ids % point_count).astype(jnp.float32) * (2.0 * math.pi / point_count)
    cosine = jnp.cos(angle)
    sine = jnp.sin(angle)
    weight = jnp.where(mode_ids == 0, 1.0, 2.0) * mode_count ** (-0.5)
    keeping = jnp.where(mode_ids == 0, 0.0, math.sqrt(mode_count) / point_count)
    synth_table = jnp.concatenate([weight * cosine, -weight * sine], axis=0)
    anal_table = jnp.concatenate([keeping * cosine, -keeping * sine], axis=0)
    return (synth_table, anal_table)


def circle_forcing(moved, synth_table, anal_table):
    columns = moved.reshape(synth_table.shape[0], -1)
    physical = lax.dot_general(synth_table, columns, (((0,), (0,)), ((), ())), precision=highest)
    squared = physical * physical
    return jnp.dot(anal_table, squared, precision=highest).reshape(moved.shape)


def damping_for(axial_int, mode_int, radial_eigen):
    axial_ids = axial_int.astype(jnp.float32) * axial_scale
    mode_ids = mode_int.astype(jnp.float32)
    return 1.0 / (
        1.0
        + viscosity * (axial_ids[None, :, None] ** 2 + mode_ids[:, None, None] ** 2)
        + radial_eigen[None, None, :]
    )


def radial_apply(rhs, analysis, synthesis, damping):
    radial_pts = rhs.shape[-1]
    coeffs = (
        jnp.dot(rhs.reshape(-1, radial_pts), analysis, precision=highest).reshape(rhs.shape)
        * damping[None]
    )
    return jnp.dot(coeffs.reshape(-1, radial_pts), synthesis, precision=highest).reshape(rhs.shape)


def window_terms(freq_list, snap_now):
    position = snap_now.astype(jnp.float32)
    window = 0.54 - 0.46 * jnp.cos(2.0 * math.pi * position / NBLK)
    phase = (freq_list * snap_now % NBLK).astype(jnp.float32) * (2.0 * math.pi / NBLK)
    return (window * jnp.cos(phase), -window * jnp.sin(phase))


def add_snapshot(block, snapshot, real_w, imag_w):
    real_new = (
        block[:, :, 0]
        + real_w[None, :, None] * snapshot[0][:, None, :]
        - imag_w[None, :, None] * snapshot[1][:, None, :]
    )
    imag_new = (
        block[:, :, 1]
        + real_w[None, :, None] * snapshot[1][:, None, :]
        + imag_w[None, :, None] * snapshot[0][:, None, :]
    )
    return jnp.stack([real_new, imag_new], axis=2)


def spectral_update(spectrum_one, old_block, new_block):
    old_real, old_imag = (old_block[:, 0], old_block[:, 1])
    new_real, new_imag = (new_block[:, 0], new_block[:, 1])
    left_real = jnp.stack([new_real, new_imag, old_real, old_imag], axis=1)
    left_imag = jnp.stack([new_imag, -new_real, old_imag, -old_real], axis=1)
    left = jnp.stack([left_real, left_imag], axis=1)
    right = jnp.stack([new_real, new_imag, -old_real, -old_imag], axis=1)
    return spectrum_one + jnp.einsum("fckr,fkq->fcrq", left, right, precision=highest)


def local(
    velocity,
    synthesis,
    analysis,
    radial_eigen,
    pair_list,
    owner_slot,
    freq_list,
    snap_index,
    block_dft,
    spectra,
):
    modes_dev = velocity.shape[1]
    axial_dev = velocity.shape[2]
    col_count = lax.axis_size("col")
    modes_all = modes_dev * col_count
    synth_table, anal_table = circle_tables(modes_all, 3 * modes_all)
    row_index = lax.axis_index("row")
    col_index = lax.axis_index("col")
    axial_int = row_index * axial_dev + jnp.arange(axial_dev, dtype=jnp.int32)
    mode_int = col_index * modes_dev + jnp.arange(modes_dev, dtype=jnp.int32)
    share = axial_dev // col_count
    state = lax.all_to_all(velocity, "col", split_axis=2, concat_axis=1, tiled=True)
    local_axial = row_index * axial_dev + col_index * share + jnp.arange(share, dtype=jnp.int32)
    local_damping = damping_for(local_axial, jnp.arange(modes_all, dtype=jnp.int32), radial_eigen)
    stepped = []
    for section_index in range(2):
        rhs = state - nonlinear_gain * circle_forcing(state, synth_table, anal_table)
        state = radial_apply(rhs, analysis, synthesis, local_damping)
        stepped.append(state)
    first, second = sent_together((stepped[0], stepped[1]), "col", 1, 2, 0)
    snapshots = [first, second]
    current = snapshots[1]
    selected = pair_list.shape[0]
    slot_ids = jnp.arange(selected, dtype=jnp.int32)
    pair_of_slot = jnp.zeros((selected,), jnp.int32).at[owner_slot].set(slot_ids)
    axial_sel = pair_list[pair_of_slot, 0]
    mode_sel = pair_list[pair_of_slot, 1]
    holder = axial_sel // axial_dev * col_count + mode_sel // modes_dev
    my_index = row_index * col_count + col_index
    both_snaps = jnp.stack(snapshots, axis=0)
    picked = both_snaps[:, :, mode_sel % modes_dev, axial_sel % axial_dev, :]
    slots_here = block_dft.shape[0]
    same_holder = holder[:, None] == holder[None, :]
    earlier = slot_ids[:, None] > slot_ids[None, :]
    position = jnp.sum(jnp.where(same_holder & earlier, 1, 0), axis=1).astype(jnp.int32)
    held_mask = holder == my_index
    hold_slots = HOLD
    placing = jnp.where(
        held_mask[None, :]
        & (position[None, :] == jnp.arange(hold_slots, dtype=jnp.int32)[:, None]),
        1.0,
        0.0,
    )
    compact = jnp.einsum("ps,abst->abpt", placing, picked, precision=highest)
    gathered = lax.all_gather(compact, ("row", "col"), axis=2, tiled=True)
    wanted = my_index * slots_here + jnp.arange(slots_here, dtype=jnp.int32)
    source = holder[wanted] * hold_slots + position[wanted]
    mine = jnp.take(gathered, source, axis=2)
    block = block_dft
    for section_index in range(2):
        real_w, imag_w = window_terms(freq_list, snap_index[0] + section_index)
        block = add_snapshot(block, mine[section_index], real_w, imag_w)
    spectra_next = jax.vmap(spectral_update)(spectra, block_dft, block)
    return (current, block, spectra_next)


def solution(mesh):
    return jax.shard_map(
        local,
        mesh=mesh,
        in_specs=(
            P(None, "col", "row", None),
            P(),
            P(),
            P(),
            P(),
            P(),
            P(),
            P(),
            P(("row", "col"), None, None, None),
            P(("row", "col"), None, None, None, None),
        ),
        out_specs=(
            P(None, "col", "row", None),
            P(("row", "col"), None, None, None),
            P(("row", "col"), None, None, None, None),
        ),
        check_vma=False,
    )
```

profile of v0, /device:TPU:1, one launch (start us, length us, event | category | flops | bytes accessed | tf_op | source)
XLA Modules:
  0.0 276.6 jit_solution(14870041637013253507)
XLA Ops:
  7.2 0.0 copy-start
  7.2 3.1 %copy.47 = f32[2,32,16,384]{3,1,0,2:T(8,128)} copy(f32[2,32,16,384]{3,2,1,0:T(8,128)} %param.10) | data formatting | bytes 3145728 | tf_op args[0]
  10.3 7.6 %all-to-all-start = ((f32[2,32,16,384]{3,1,0,2:T(8,128)}), f32[2,32,16,384]{3,1,0,2:T(8,128)S(1)}, u32[]{:S(2)}, u32[]{:S(2)}) async-start(f32[2,32,16,384]{3,1,0,2:T(8,128)} %copy.47), calls=%async_computation | async-start | bytes 3145728 | tf_op jit(solution)/shard_map/all_to_all | solution.py:123
  18.0 0.2 add_divide_fusion
  18.2 14.2 %fusion.12 = (f32[512,1536]{1,0:T(8,128)}, f32[512,1536]{1,0:T(8,128)}) fusion(f32[512]{0:T(512)S(1)} %select_multiply_fusion, f32[512]{0:T(512)S(1)} %fusion.55), kind=kLoop, calls=%fused_computation.27 | loop fusion | flops 8650752 | bytes 6295552 | tf_op jit(solution)/shard_map/mul | solution.py:39
  32.4 14.7 %fusion.13 = (f32[512,1536]{1,0:T(8,128)}, f32[512,1536]{1,0:T(8,128)}) fusion(f32[512]{0:T(512)S(1)} %fusion.43, f32[512]{0:T(512)S(1)} %fusion.54), kind=kLoop, calls=%fused_computation.28 | loop fusion | flops 8650752 | bytes 6295552 | tf_op jit(solution)/shard_map/mul | solution.py:40
  47.1 0.0 copy-start.6
  47.1 0.1 copy.48
  47.2 1.8 copy-done.6
  49.0 12.0 %fusion.4 = f32[1536,384]{1,0:T(8,128)S(1)} fusion(f32[1024,384]{1,0:T(8,128)S(1)} %bitcast.85, f32[512,1536]{1,0:T(8,128)} %get-tuple-element.48, f32[512,1536]{1,0:T(8,128)S(1)} %copy-done.6), kind=kOutput, calls=%fused_computation.15 | convolution fusion | flops 7249920000 | bytes 10223616 | tf_op jit(solution)/shard_map/dot_general | solution.py:46
  61.0 10.1 %multiply_subtract_fusion.1 = f32[1024,384]{1,0:T(8,128)S(1)} fusion(f32[1024,384]{1,0:T(8,128)S(1)} %bitcast.86, f32[1536,384]{1,0:T(8,128)S(1)} %fusion.4, f32[512,1536]{1,0:T(8,128)S(1)} %copy-done.4, f32[512,1536]{1,0:T(8,128)S(1)} %copy-done.3), kind=kOutput, calls=%fused_computation.38 | convolution fusion | flops 7250116608 | bytes 11796480 | tf_op jit(solution)/shard_map/dot_general | solution.py:48
  71.1 0.0 copy-start.8
  71.2 3.2 %convolution_multiply_fusion = f32[2,512,384]{2,1,0:T(8,128)S(1)} fusion(f32[2,512,384]{2,1,0:T(8,128)S(1)} %bitcast.87, f32[512,384]{1,0:T(8,128)S(1)} %add_divide_fusion, f32[384,384]{1,0:T(8,128)S(1)} %copy-done), kind=kOutput, calls=%fused_computation.40 | convolution fusion | flops 1812332544 | bytes 4521984 | tf_op jit(solution)/shard_map/dot_general | solution.py:64
  74.4 3.2 %fusion.77 = f32[1024,384]{1,0:T(8,128)S(1)} fusion(f32[1024,384]{1,0:T(8,128)S(1)} %bitcast.83, f32[384,384]{1,0:T(8,128)S(1)} %copy-done.8), kind=kOutput, calls=%fused_computation.149 | convolution fusion | flops 1811939328 | bytes 3735552 | tf_op jit(solution)/shard_map/dot_general | solution.py:67
  77.6 10.0 %fusion.5 = f32[1536,384]{1,0:T(8,128)S(1)} fusion(f32[1024,384]{1,0:T(8,128)S(1)} %fusion.77, f32[512,1536]{1,0:T(8,128)S(1)} %copy-done.7, f32[512,1536]{1,0:T(8,128)S(1)} %copy-done.6), kind=kOutput, calls=%fused_computation.16 | convolution fusion | flops 7249920000 | bytes 10223616 | tf_op jit(solution)/shard_map/dot_general | solution.py:46
  87.6 10.4 %multiply_subtract_fusion = f32[1024,384]{1,0:T(8,128)S(1)} fusion(f32[1024,384]{1,0:T(8,128)S(1)} %fusion.77, f32[1536,384]{1,0:T(8,128)S(1)} %fusion.5, f32[512,1536]{1,0:T(8,128)S(1)} %copy-done.4, f32[512,1536]{1,0:T(8,128)S(1)} %copy-done.3), kind=kOutput, calls=%fused_computation.37 | convolution fusion | flops 7250116608 | bytes 11796480 | tf_op jit(solution)/shard_map/dot_general | solution.py:48
  98.0 3.2 %fusion.29 = f32[2,512,384]{2,1,0:T(8,128)S(1)} fusion(f32[2,512,384]{2,1,0:T(8,128)S(1)} %bitcast.84, f32[384,384]{1,0:T(8,128)S(1)} %copy-done), kind=kOutput, calls=%fused_computation.47 | convolution fusion | flops 1811939328 | bytes 3735552 | tf_op jit(solution)/shard_map/dot_general | solution.py:64
  101.2 3.2 %fusion.21 = f32[2,512,1,384]{3,1,0,2:T(8,128)S(1)} fusion(f32[2,512,384]{2,1,0:T(8,128)S(1)} %fusion.29, f32[512,384]{1,0:T(8,128)S(1)} %add_divide_fusion, f32[384,384]{1,0:T(8,128)S(1)} %copy-done.8), kind=kOutput, calls=%fused_computation.39 | convolution fusion | flops 1812332544 | bytes 4521984 | tf_op jit(solution)/shard_map/dot_general | solution.py:67
  104.4 0.2 pad_maximum_fusion.10
  104.7 3.7 %copy.49 = f32[4,512,1,384]{3,0,2,1:T(4,128)} copy(f32[4,512,1,384]{3,1,0,2:T(8,128)S(1)} %pad_maximum_fusion.10) | data formatting | bytes 6291456 | tf_op jit(solution)/shard_map/concatenate | solution.py:19
  108.3 6.8 %all-to-all-start.1 = ((f32[4,512,1,384]{3,0,2,1:T(4,128)}), f32[4,512,1,384]{3,0,2,1:T(4,128)S(1)}, u32[]{:S(2)}, u32[]{:S(2)}) async-start(f32[4,512,1,384]{3,0,2,1:T(4,128)} %copy.49), calls=%async_computation.1 | async-start | bytes 6291456 | tf_op jit(solution)/shard_map/all_to_all | solution.py:21
  115.1 0.0 all-gather.2.cloned.1.call-start
  115.2 1.4 scatter_custom_fusion
  116.6 2.5 gather_fusion.1
  119.1 2.5 gather_fusion
  121.6 0.2 select_reduce_fusion
  121.8 33.5 %all-to-all-done.1 = f32[4,512,1,384]{3,0,2,1:T(4,128)S(1)} async-done(((f32[4,512,1,384]{3,0,2,1:T(4,128)}), f32[4,512,1,384]{3,0,2,1:T(4,128)S(1)}, u32[]{:S(2)}, u32[]{:S(2)}) %all-to-all-start.1) | async-done | bytes 3145760 | tf_op jit(solution)/shard_map/all_to_all | solution.py:21
  155.4 0.9 copy.84
  156.2 2.9 %slice_bitcast_fusion = (f32[1,2,32,16,384]{4,1,3,2,0:T(2,128)S(1)}, f32[1,2,32,16,384]{4,1,3,2,0:T(2,128)S(1)}, f32[2,32,16,384]{3,0,2,1:T(2,128)}) fusion(f32[4,32,16,1,384]{4,0,2,1,3:T(4,128)S(1)} %bitcast.80), kind=kLoop, calls=%fused_computation.32 | loop fusion | bytes 7864320 | tf_op jit(solution)/shard_map/stack | solution.py:141
  159.1 1.6 pad_maximum_fusion.11
  160.8 0.0 copy-start.9
  160.8 0.0 copy-start.12
  160.8 3.7 %gather_fusion.4 = f32[256,2,2,384]{3,2,1,0:T(2,128)} fusion(f32[2,2,32,16,384]{4,1,3,2,0:T(2,128)S(1)} %pad_maximum_fusion.11, s32[256]{0:T(256)S(1)} %bitcast.77), kind=kCustom, calls=%fused_computation.4 | custom fusion | bytes 3147776 | tf_op jit(solution)/shard_map/gather | solution.py:142
  164.5 3.1 %fusion.24 = f32[2,2,8,384]{3,2,1,0:T(8,128)} fusion(f32[2,2,256,384]{3,1,0,2:T(2,128)} %bitcast.82, s32[256]{0:T(256)S(1)} %select_reduce_fusion, pred[256]{0:T(512)(128)(4,1)S(1)} %get-tuple-element.24), kind=kOutput, calls=%fused_computation.43 | convolution fusion | flops 37754880 | bytes 1623296 | tf_op jit(solution)/shard_map/ps,abst->abpt/dot_general | solution.py:155
  167.6 0.0 all-gather.2.cloned.1.call-update
  167.7 0.6 gather_fusion.3
  168.3 0.6 gather_fusion.2
  169.8 0.1 cosine_multiply_fusion.1
  169.9 0.1 sine_multiply_fusion
  170.0 1.3 copy.59
  171.2 69.5 %all-gather.2.cloned.1.call-done = f32[2,2,1024,384]{3,2,1,0:T(8,128)} async-done(((f32[2,2,8,384]{3,2,1,0:T(8,128)}), f32[2,2,1024,384]{3,2,1,0:T(8,128)}) %all-gather.2.cloned.1.call-update) | async-done | bytes 6291472 | tf_op jit(solution)/shard_map/all_gather | solution.py:156
  240.7 10.5 %copy.54 = f32[2,2,1024,384]{3,1,2,0:T(2,128)} copy(f32[2,2,1024,384]{3,2,1,0:T(8,128)} %all-gather.2.cloned.1.call-done) | data formatting | bytes 12582912 | tf_op jit(solution)/shard_map/all_gather | solution.py:156
  251.3 3.4 %gather_fusion.5 = f32[2,2,2,384]{3,2,1,0:T(2,128)S(1)} fusion(f32[2,2,1024,384]{3,1,2,0:T(2,128)} %copy.54, s32[1024]{0:T(1024)S(1)} %pad_clamp_fusion), kind=kCustom, calls=%fused_computation.5 | custom fusion | bytes 24584 | tf_op jit(solution)/shard_map/jit(_take)/gather | solution.py:159
  254.6 0.1 select_bitcast_fusion
  254.8 0.1 slice_negate_fusion.1
  254.9 0.6 copy.60
  255.6 0.0 copy-start.1
  255.6 14.0 %convolution_add_fusion = f32[2,4,2,384,384]{4,3,2,1,0:T(8,128)} fusion(f32[2,4,2,384,384]{4,3,2,1,0:T(8,128)} %param.19, f32[2,4,2,4,384]{4,1,3,0,2:T(4,128)S(1)} %pad_maximum_fusion.16, f32[2,4,4,384,1]{3,1,2,0,4:T(4,128)S(1)} %get-tuple-element.30), kind=kOutput, calls=%fused_computation.14 | convolution fusion | flops 115605504 | bytes 19021824 | tf_op jit(solution)/shard_map/vmap(fckr,fkq->fcrq)/dot_general | solution.py:98
  (44 shorter events, 0.2 us)
Async XLA Ops:
  7.2 64.0 %copy-start = (f32[384,384]{1,0:T(8,128)S(1)}, f32[384,384]{1,0:T(8,128)}, u32[]{:S(2)}) copy-start(f32[384,384]{1,0:T(8,128)} %param.12) | copy-start | bytes 1769476
  7.2 10.8 %copy-start.10 = (f32[384]{0:T(512)S(1)}, f32[384]{0:T(512)}, u32[]{:S(2)}) copy-start(f32[384]{0:T(512)} %param.13) | copy-start | bytes 4612
  10.3 36.8 %all-to-all-start = ((f32[2,32,16,384]{3,1,0,2:T(8,128)}), f32[2,32,16,384]{3,1,0,2:T(8,128)S(1)}, u32[]{:S(2)}, u32[]{:S(2)}) async-start(f32[2,32,16,384]{3,1,0,2:T(8,128)} %copy.47), calls=%async_computation | async-start | bytes 3145728 | tf_op jit(solution)/shard_map/all_to_all | solution.py:123
  47.1 1.9 copy-start.6
  49.0 12.0 %copy-start.3 = (f32[512,1536]{1,0:T(8,128)S(1)}, f32[512,1536]{1,0:T(8,128)}, u32[]{:S(2)}) copy-start(f32[512,1536]{1,0:T(8,128)} %get-tuple-element.49) | copy-start | bytes 9437188
  49.0 12.0 %copy-start.4 = (f32[512,1536]{1,0:T(8,128)S(1)}, f32[512,1536]{1,0:T(8,128)}, u32[]{:S(2)}) copy-start(f32[512,1536]{1,0:T(8,128)} %get-tuple-element.50) | copy-start | bytes 9437188
  71.1 3.2 %copy-start.8 = (f32[384,384]{1,0:T(8,128)S(1)}, f32[384,384]{1,0:T(8,128)}, u32[]{:S(2)}) copy-start(f32[384,384]{1,0:T(8,128)} %param.11) | copy-start | bytes 1769476
  71.1 6.5 %copy-start.7 = (f32[512,1536]{1,0:T(8,128)S(1)}, f32[512,1536]{1,0:T(8,128)}, u32[]{:S(2)}) copy-start(f32[512,1536]{1,0:T(8,128)} %get-tuple-element.48) | copy-start | bytes 9437188
  108.3 6.8 %copy-start.11 = (s32[256]{0:T(256)S(1)}, s32[256]{0:T(256)}, u32[]{:S(2)}) copy-start(s32[256]{0:T(256)} %param.15) | copy-start | bytes 3076
  108.3 8.3 %copy-start.2 = (s32[256,2]{0,1:T(2,128)S(1)}, s32[256,2]{0,1:T(2,128)}, u32[]{:S(2)}) copy-start(s32[256,2]{0,1:T(2,128)} %param.14) | copy-start | bytes 6148
  108.3 47.0 %all-to-all-start.1 = ((f32[4,512,1,384]{3,0,2,1:T(4,128)}), f32[4,512,1,384]{3,0,2,1:T(4,128)S(1)}, u32[]{:S(2)}, u32[]{:S(2)}) async-start(f32[4,512,1,384]{3,0,2,1:T(4,128)} %copy.49), calls=%async_computation.1 | async-start | bytes 6291456 | tf_op jit(solution)/shard_map/all_to_all | solution.py:21
  115.1 125.6 %all-gather.2.cloned.1.call-start = ((), (), s32[]{:S(2)}) async-start(), calls=%async_computation.2 | async-start | bytes 6340608 | tf_op jit(solution)/shard_map/all_gather | solution.py:156
  160.8 9.0 %copy-start.9 = (f32[2,4,2,384]{3,2,1,0:T(2,128)S(1)}, f32[2,4,2,384]{3,2,1,0:T(2,128)}, u32[]{:S(2)}) copy-start(f32[2,4,2,384]{3,2,1,0:T(2,128)} %param.18) | copy-start | bytes 73732
  160.8 9.0 %copy-start.12 = (s32[4]{0:T(128)S(1)}, s32[4]{0:T(128)}, u32[]{:S(2)}) copy-start(s32[4]{0:T(128)} %param.16) | copy-start | bytes 52
  164.5 5.4 %copy-start.5 = (f32[2,32,16,384]{3,0,2,1:T(2,128)S(1)}, f32[2,32,16,384]{3,0,2,1:T(2,128)}, u32[]{:S(2)}) copy-start(f32[2,32,16,384]{3,0,2,1:T(2,128)} %get-tuple-element.28) | copy-start | bytes 4718596
  255.6 14.0 %copy-start.1 = (f32[384,384]{1,0:T(8,128)S(1)}, f32[384,384]{1,0:T(8,128)}, u32[]{:S(2)}) copy-start(f32[384,384]{1,0:T(8,128)} %param.12) | copy-start | bytes 1769476
Sparse Core Ops, SparseCore 0:
  167.8 72.9 all-gather.1
where the time goes:
time: 280 us; the launch traced here: 277 us
  waiting for transfers between devices  103 us (37%)
  matrix products  72.4 us (26%)
  local copies, waits for them, and re-layouts  39.7 us (14%)
  other arithmetic  31.6 us (11%)
  between operations  15.6 us (6%)
  starting transfers between devices  14.4 us (5%)
    all_gather x1, waiting for transfers between devices, local(): gathered = lax.all_gather(compact, ('row', 'col'), axis=2, tiled=True)  69.5 us
    all_to_all x1, waiting for transfers between devices, sent_together(): lax.all_to_all(both, axis, split_axis=split_dim, concat_axis=concat_dim,...  33.5 us
    dot_general x2, matrix products, circle_forcing(): lax.dot_general(synth_table, columns, (((0,), (0,)), ((), ())), precision...  22 us
    dot_general x2, matrix products, circle_forcing(): return jnp.dot(anal_table, squared, precision=highest).reshape(moved.shape)  20.5 us
    mul x1, other arithmetic, circle_tables(): anal_table = jnp.concatenate([keeping * cosine, -keeping * sine], axis=0)  14.7 us
    mul x1, other arithmetic, circle_tables(): synth_table = jnp.concatenate([weight * cosine, -weight * sine], axis=0)  14.2 us
    dot_general x1, matrix products, spectral_update(): jnp.einsum('fckr,fkq->fcrq', left, right, precision=highest)  14 us
    all_gather x1, local copies, waits for them, and re-layouts, local(): gathered = lax.all_gather(compact, ('row', 'col'), axis=2, tiled=True)  10.5 us
  transfers between devices with their start and end apart: 3, of which 2 were waited for; matrix products, arithmetic and copies ran while one was open for 14% of the time, Pallas kernels for 0%

commit v1 on v0

v1 whole, which is shorter than its diff:
```python
import math

import jax
import jax.numpy as jnp
from jax import lax
from jax.experimental import pallas as pl
from jax.experimental.pallas import tpu as pltpu
from jax.sharding import PartitionSpec as P


NBLK = 256
MTH = 512
NTH = 1536
NR = 384
HALF = MTH // 2
QUARTER = NTH // 4

viscosity = 4e-06
axial_scale = 2.0
nonlinear_gain = 0.1

f32 = jnp.float32
bf16 = jnp.bfloat16


SYNTH_WEIGHT = 2.0 / math.sqrt(MTH)
KEEP = math.sqrt(MTH) / NTH
VMEM = pl.BlockSpec(memory_space=pltpu.VMEM)
SMEM = pl.BlockSpec(memory_space=pltpu.SMEM)
HBM = pl.BlockSpec(memory_space=pltpu.HBM)
ANY = pl.BlockSpec(memory_space=pl.ANY)


def in_hbm(array):
    return pltpu.with_memory_space_constraint(array, pltpu.HBM)


def params(mib):
    return pltpu.CompilerParams(vmem_limit_bytes=mib << 20)


def trig_tables(transposed):
    dims = (4, HALF, QUARTER) if transposed else (4, QUARTER, HALF)
    mode_dim, point_dim = (1, 2) if transposed else (2, 1)
    kind = lax.broadcasted_iota(jnp.int32, dims, 0)
    mode = (2 * lax.broadcasted_iota(jnp.int32, dims, mode_dim) + (kind & 1)).astype(f32)
    point = (2 * lax.broadcasted_iota(jnp.int32, dims, point_dim) + 1).astype(f32)
    product = mode * point - jnp.where(kind >= 2, NTH / 2.0, 0.0)
    turn = product - jnp.round(product * (0.5 / NTH)) * (2.0 * NTH)
    quarter = (NTH / 2.0 - jnp.abs(turn)) * (math.pi / NTH)
    square = quarter * quarter
    series = 1.0 / math.factorial(13)
    for power in (11, 9, 7, 5, 3, 1):
        series = (1.0 if power % 4 == 1 else -1.0) / math.factorial(power) + square * series
    table = quarter * series
    high = lax.reduce_precision(table, 8, 7)
    low = table - high
    high, low = high.astype(bf16), low.astype(bf16)
    return high, low


def gather_kernel(src_ref, out_ref):
    for parity in range(2):
        block = jnp.stack([src_ref[0, 2 * i + parity] for i in range(8)])
        out_ref[:, parity * 8 : parity * 8 + 8, :] = pltpu.einshape("mar->amr", block)


def to_axial_major(velocity):
    return pl.pallas_call(
        gather_kernel,
        out_shape=jax.ShapeDtypeStruct((16, 64, NR), f32),
        grid=(2, 2),
        in_specs=[pl.BlockSpec((1, 16, 16, NR), lambda c, i: (c, i, 0, 0))],
        out_specs=pl.BlockSpec((16, 16, NR), lambda c, i: (0, 2 * c + i, 0)),
        compiler_params=params(8),
        cost_estimate=pl.CostEstimate(flops=0, bytes_accessed=2 * 1024 * NR * 4, transcendentals=0),
        name="axial_major",
    )(in_hbm(velocity))


def scatter_kernel(src_ref, out_ref):
    for parity in range(2):
        block = src_ref[:, parity * 8 : parity * 8 + 8, :]
        moved = pltpu.einshape("amr->mar", block)
        for i in range(8):
            out_ref[0, 2 * i + parity] = moved[i]


def from_axial_major(moved):
    return pl.pallas_call(
        scatter_kernel,
        out_shape=jax.ShapeDtypeStruct((2, 32, 16, NR), f32),
        grid=(2, 2),
        in_specs=[pl.BlockSpec((16, 16, NR), lambda c, i: (0, 2 * c + i, 0))],
        out_specs=pl.BlockSpec((1, 16, 16, NR), lambda c, i: (c, i, 0, 0)),
        compiler_params=params(8),
        cost_estimate=pl.CostEstimate(flops=0, bytes_accessed=2 * 1024 * NR * 4, transcendentals=0),
        name="mode_major",
    )(moved)


def list_kernel(pair_ref, owner_ref, place_ref, count_ref, spot_ref, mode_ref):
    mine, core, z, x, y = (place_ref[i] for i in range(5))

    def eight(b, n):
        for u in range(8):
            mode_ref[n] = b * 8 + u
            n = n + jnp.where(pair_ref[0, b * 8 + u] == mine, 1, 0)
        return n

    def place_one(k, carry):
        i = mode_ref[k]
        slot = owner_ref[i]
        row, col = slot // 32, (slot // 2) & 15
        spot_ref[k] = (
            ((row & 1) ^ core) * 128
            + (((row >> 1) - z) & 3) * 32
            + (((col >> 2) - x) & 3) * 8
            + (((col & 3) - y) & 3) * 2
            + (slot & 1)
        )
        mode_ref[k] = pair_ref[1, i]
        return carry

    count = lax.fori_loop(0, 32, eight, 0)
    count_ref[0] = count
    lax.fori_loop(0, count, place_one, 0)


def pair_lists(pair_list, owner_slot, place):
    return pl.pallas_call(
        list_kernel,
        out_shape=(
            jax.ShapeDtypeStruct((1,), jnp.int32),
            jax.ShapeDtypeStruct((257,), jnp.int32),
            jax.ShapeDtypeStruct((257,), jnp.int32),
        ),
        in_specs=[SMEM] * 3,
        out_specs=[SMEM] * 3,
        compiler_params=params(1),
        cost_estimate=pl.CostEstimate(flops=0, bytes_accessed=8000000, transcendentals=0),
        name="pair_lists",
    )(pair_list.T, owner_slot, place)


def split(value):
    high = value.astype(bf16)
    return high, (value - high.astype(f32)).astype(bf16)


BANDS = ((0, 256), (256, 128))


def steps_kernel(
    count_ref,
    spot_ref,
    mode_ref,
    moved_any,
    synth_any,
    anal_any,
    analysis_any,
    synthesis_any,
    damp_any,
    out_any,
    keep_any,
    send_any,
    state,
    synth_ref,
    anal_ref,
    analysis_ref,
    synthesis_ref,
    damp_ref,
    cols,
    phys,
    squares,
    rows,
    parcel,
    sems,
):
    def strip(array, part, half):
        return array.at[:, pl.ds((part // 2) * 32 + half * 16 + (part % 2) * 8, 8), :]

    def held(part, half):
        return state.at[part, :, pl.ds(half * 8, 8), :]

    moved_in = [
        [
            pltpu.make_async_copy(strip(moved_any, part, half), held(part, half), sems.at[2 * part + half])
            for half in range(2)
        ]
        for part in range(4)
    ]
    synth_in = [
        pltpu.make_async_copy(synth_any.at[part], synth_ref.at[part], sems.at[8 + part]) for part in range(4)
    ]
    anal_in = [pltpu.make_async_copy(anal_any.at[part], anal_ref.at[part], sems.at[12 + part]) for part in range(4)]
    rest_in = [
        pltpu.make_async_copy(analysis_any, analysis_ref, sems.at[16]),
        pltpu.make_async_copy(damp_any, damp_ref, sems.at[17]),
        pltpu.make_async_copy(synthesis_any, synthesis_ref, sems.at[18]),
    ]
    for part in range(4):
        for copy in moved_in[part]:
            copy.start()
        synth_in[part].start()
    for copy in anal_in + rest_in:
        copy.start()
    parcel[...] = jnp.zeros_like(parcel)

    def store_rows(at, lanes, value):
        high, low = split(value)
        start, width = lanes
        rows[at, start : start + width] = high
        rows[at, NR + start : NR + start + width] = low
        rows[at, 2 * NR + start : 2 * NR + start + width] = high

    def step(t, carry):
        for start, width in BANDS:
            lanes = pl.ds(start, width)
            for part in range(4):
                if start == 0:

                    @pl.when(t == 0)
                    def _():
                        for copy in moved_in[part]:
                            copy.wait()
                        synth_in[part].wait()

                for b in range(0, HALF, 64):
                    scaled = state[part, pl.ds(b // 16, 4), :, lanes].reshape(64, width) * SYNTH_WEIGHT
                    if part == 0 and b == 0:
                        first_row = lax.broadcasted_iota(jnp.int32, scaled.shape, 0) == 0
                        scaled = jnp.where(first_row, 0.5 * scaled, scaled)
                    high, low = split(scaled)
                    cols[part, pl.ds(b, 64), lanes] = high
                    cols[part, pl.ds(HALF + b, 64), lanes] = low
                    cols[part, pl.ds(2 * HALF + b, 64), lanes] = high
                phys[part, :, lanes] = jnp.dot(synth_ref[part], cols[part, :, lanes], preferred_element_type=f32)

        @pl.when(t == 0)
        def _():
            for copy in anal_in + rest_in:
                copy.wait()

        for start, width in BANDS:
            lanes = pl.ds(start, width)
            for b in range(0, QUARTER, 32):
                ce, co, se, so = (phys[part, pl.ds(b, 32), lanes] for part in range(4))
                a, b_, s, d = ce + co, ce - co, se + so, se - so
                near, far = a * a + s * s, b_ * b_ + d * d
                near_x, far_x = a * s, b_ * d
                for part, value in enumerate((near + far, near - far, near_x + far_x, near_x - far_x)):
                    high, low = split(value)
                    squares[part, pl.ds(b, 32), lanes] = high
                    squares[part, pl.ds(QUARTER + b, 32), lanes] = low
                    squares[part, pl.ds(2 * QUARTER + b, 32), lanes] = high
            for part in range(4):
                folded = jnp.dot(anal_ref[part], squares[part, :, lanes], preferred_element_type=f32)
                gain = -nonlinear_gain * KEEP * (2.0 if part < 2 else 4.0)
                if part == 0:
                    first_row = lax.broadcasted_iota(jnp.int32, folded.shape, 0) == 0
                    folded = jnp.where(first_row, 0.0, folded)
                old = state[part, :, :, lanes].reshape(HALF, width)
                store_rows(pl.ds(part * HALF, HALF), (start, width), old + gain * folded)
        for half in range(2):
            at = pl.ds(half * MTH, MTH)
            coeffs = jnp.dot(rows[at, :], analysis_ref[...], preferred_element_type=f32)
            store_rows(at, (0, NR), coeffs * damp_ref[...])
        for half in range(2):
            at = pl.ds(half * MTH, MTH)
            value = jnp.dot(rows[at, :], synthesis_ref[...], preferred_element_type=f32)
            state[pl.ds(2 * half, 2)] = value.reshape(2, 16, 16, NR)
        return carry

    def pick(t):
        def one(i, carry):
            mode = mode_ref[i]
            part, group, row = mode & 1, (mode >> 1) >> 4, (mode >> 1) & 15
            dst = spot_ref[i] * 4 + 2 * t
            parcel[pl.ds(dst, 1), :] = state[part, group, pl.ds(row, 1), :]
            parcel[pl.ds(dst + 1, 1), :] = state[part + 2, group, pl.ds(row, 1), :]
            return carry

        lax.fori_loop(0, count_ref[0], one, 0)

    def step_and_pick(t, carry):
        step(t, 0)
        pick(t)
        return carry

    lax.fori_loop(0, 2, step_and_pick, 0)
    copies = [
        pltpu.make_async_copy(held(part, half), strip(out_any, part, half), sems.at[2 * part + half])
        for part in range(4)
        for half in range(2)
    ]
    copies.append(pltpu.make_async_copy(parcel.at[pl.ds(512, 512)], send_any, sems.at[8]))
    copies.append(pltpu.make_async_copy(parcel.at[pl.ds(0, 512)], keep_any, sems.at[9]))
    for copy in copies:
        copy.start()
    for copy in copies:
        copy.wait()


def two_steps(lists, moved, synth, anal, analysis, synthesis, damping):
    return pl.pallas_call(
        steps_kernel,
        out_shape=(
            pltpu.HBM((16, 64, NR), f32),
            pltpu.HBM((512, NR), f32),
            pltpu.HBM((512, NR), f32),
        ),
        in_specs=[SMEM] * 3 + [ANY] + [HBM] * 5,
        out_specs=[HBM, HBM, HBM],
        scratch_shapes=[
            pltpu.VMEM((4, 16, 16, NR), f32),
            pltpu.VMEM((4, QUARTER, 3 * HALF), bf16),
            pltpu.VMEM((4, HALF, 3 * QUARTER), bf16),
            pltpu.VMEM((3 * NR, NR), bf16),
            pltpu.VMEM((3 * NR, NR), bf16),
            pltpu.VMEM((MTH, NR), f32),
            pltpu.VMEM((4, 3 * HALF, NR), bf16),
            pltpu.VMEM((4, QUARTER, NR), f32),
            pltpu.VMEM((4, 3 * QUARTER, NR), bf16),
            pltpu.VMEM((1024, 3 * NR), bf16),
            pltpu.VMEM((1024, NR), f32),
            pltpu.SemaphoreType.DMA((19,)),
        ],
        compiler_params=params(40),
        cost_estimate=pl.CostEstimate(flops=8_000_000_000, bytes_accessed=10_000_000, transcendentals=0),
        name="two_steps",
    )(*lists, moved, *map(in_hbm, (synth, anal, analysis, synthesis, damping)))


def products(lefts, rights, left, right):
    def three(value):
        high = value.astype(bf16).astype(f32)
        middle = (value - high).astype(bf16).astype(f32)
        return high, middle, (value - high - middle).astype(bf16).astype(f32)

    pairs = ((0, 0), (0, 1), (1, 0), (1, 1), (0, 2), (2, 0))
    left[...] = jnp.zeros_like(left)
    right[...] = jnp.zeros_like(right)
    count = len(rights)
    for k in range(count):
        for part in range(2):
            pieces = three(lefts[k][part])
            for p, (i, _) in enumerate(pairs):
                left[p * count + k : p * count + k + 1, part * NR : (part + 1) * NR] = pieces[i]
        pieces = three(rights[k])
        for p, (_, i) in enumerate(pairs):
            right[p * count + k : p * count + k + 1, :] = pieces[i]
    r = right[...].astype(bf16)
    for part in range(2):
        l = left[:, part * NR : (part + 1) * NR].T.astype(bf16)
        yield part, jnp.dot(l, r, preferred_element_type=f32)


def retire_kernel(block_ref, spectra_ref, out_ref, left, right):
    step = pl.program_id(0)
    real, imag = block_ref[0, 0:1, :], block_ref[0, 1:2, :]
    for part, value in products(((real, imag), (imag, -real)), (real, imag), left, right):
        out_ref[step, part] = spectra_ref[0, part] - value


def retire_old(block_dft, spectra):
    return pl.pallas_call(
        retire_kernel,
        out_shape=jax.ShapeDtypeStruct((8, 2, NR, NR), f32),
        grid=(8,),
        in_specs=[
            pl.BlockSpec((1, 2, NR), lambda i: (i, 0, 0)),
            pl.BlockSpec((1, 2, NR, NR), lambda i: (i, 0, 0, 0)),
        ],
        out_specs=VMEM,
        scratch_shapes=[pltpu.VMEM((16, 2 * NR), f32), pltpu.VMEM((16, NR), f32)],
        compiler_params=params(16),
        cost_estimate=pl.CostEstimate(flops=300_000_000, bytes_accessed=19_000_000, transcendentals=0),
        name="retire_old",
    )(block_dft.reshape(8, 2, NR), in_hbm(spectra.reshape(8, 2, NR, NR)))


def admit_kernel(weight_ref, snap_ref, block_ref, retired_ref, sums_ref, out_any, spread, sems):
    real, imag = block_ref[:, 0, :], block_ref[:, 1, :]
    for t in range(2):
        real_w, imag_w = weight_ref[:, 2 * t : 2 * t + 1], weight_ref[:, 2 * t + 1 : 2 * t + 2]
        snap_real, snap_imag = (
            jnp.concatenate(
                [
                    jnp.broadcast_to(snap_ref[slot * 4 + 2 * t + c : slot * 4 + 2 * t + c + 1, :], (4, NR))
                    for slot in range(2)
                ],
                axis=0,
            )
            for c in range(2)
        )
        real, imag = (
            real + real_w * snap_real - imag_w * snap_imag,
            imag + real_w * snap_imag + imag_w * snap_real,
        )
    sums_ref[:, 0, :] = real
    sums_ref[:, 1, :] = imag
    real_cols, imag_cols = real.T, imag.T
    copies = []
    rows = NR // 2
    for i in range(8):
        for half in range(2):
            n = 2 * i + half
            held = n % 8
            if n >= 8:
                copies[n - 8].wait()
            for b in range(0, rows, 32):
                at, here = pl.ds(half * rows + b, 32), pl.ds(b, 32)
                cr = real_cols[half * rows + b : half * rows + b + 32, i : i + 1]
                ci = imag_cols[half * rows + b : half * rows + b + 32, i : i + 1]
                rr, ri = real[i : i + 1, :], imag[i : i + 1, :]
                spread[held, 0, here, :] = retired_ref[i, 0, at, :] + (cr * rr + ci * ri)
                spread[held, 1, here, :] = retired_ref[i, 1, at, :] + (ci * rr - cr * ri)
            copies.append(
                pltpu.make_async_copy(
                    spread.at[held], out_any.at[i, :, pl.ds(half * rows, rows), :], sems.at[n]
                )
            )
            copies[n].start()
    for n in range(8, 16):
        copies[n].wait()


def admit_new(weights, snaps, block_dft, retired):
    sums, out = pl.pallas_call(
        admit_kernel,
        out_shape=(
            jax.ShapeDtypeStruct((8, 2, NR), f32),
            jax.ShapeDtypeStruct((8, 2, NR, NR), f32),
        ),
        in_specs=[VMEM] * 4,
        out_specs=[VMEM, ANY],
        scratch_shapes=[pltpu.VMEM((8, 2, NR // 2, NR), f32), pltpu.SemaphoreType.DMA((16,))],
        compiler_params=params(8),
        cost_estimate=pl.CostEstimate(flops=300_000_000, bytes_accessed=10_000_000, transcendentals=0),
        name="admit_new",
    )(weights, snaps, block_dft.reshape(8, 2, NR), retired)
    return sums.reshape(2, 4, 2, NR), out.reshape(2, 4, 2, NR, NR)


def window_terms(freq_list, snap_now):
    position = snap_now.astype(f32)
    window = 0.54 - 0.46 * jnp.cos(2.0 * math.pi * position / NBLK)
    phase = (freq_list * snap_now % NBLK).astype(f32) * (2.0 * math.pi / NBLK)
    return (window * jnp.cos(phase), -window * jnp.sin(phase))


def route(keep, send):
    rows = [[z * 2 + c for c in range(2)] for z in range(4)]
    got = lax.ppermute(send, "row", [(i, i ^ 1) for i in range(8)])
    z_size = 128
    blocks = [keep[k * z_size : (k + 1) * z_size] + got[k * z_size : (k + 1) * z_size] for k in range(4)]

    def turn(blocks, axis, pairs_of):
        total = blocks[0]
        for k in range(1, 4):
            moved = lax.ppermute(blocks[k], axis, pairs_of(k))
            total = total + moved
        return total

    total = turn(blocks, "row", lambda k: [(rows[z][c], rows[(z + k) % 4][c]) for z in range(4) for c in range(2)])
    blocks = [total[k * 32 : (k + 1) * 32] for k in range(4)]
    total = turn(blocks, "col", lambda k: [(x * 4 + y, (x + k) % 4 * 4 + y) for x in range(4) for y in range(4)])
    blocks = [total[k * 8 : (k + 1) * 8] for k in range(4)]
    snaps = turn(blocks, "col", lambda k: [(x * 4 + y, x * 4 + (y + k) % 4) for x in range(4) for y in range(4)])
    return snaps


def local(
    velocity,
    synthesis,
    analysis,
    radial_eigen,
    pair_list,
    owner_slot,
    freq_list,
    snap_index,
    block_dft,
    spectra,
):
    row_index = lax.axis_index("row")
    col_index = lax.axis_index("col")
    mine = row_index * 16 + col_index
    moved = lax.all_to_all(to_axial_major(velocity), "col", split_axis=0, concat_axis=0, tiled=True)

    high, low = trig_tables(False)
    synth = jnp.concatenate([high, high, low], axis=2)
    high, low = trig_tables(True)
    anal = jnp.concatenate([high, high, low], axis=2)

    def stacked(matrix):
        high = lax.reduce_precision(matrix, 8, 7)
        low = matrix - high
        high, low = high.astype(bf16), low.astype(bf16)
        return jnp.concatenate([high, high, low], axis=0)

    parity = jnp.arange(2, dtype=jnp.int32)[:, None, None]
    mode_ids = (2 * jnp.arange(HALF, dtype=jnp.int32)[None, :, None] + parity).astype(f32)
    axial_id = mine.astype(f32) * axial_scale
    damping = 1.0 / (
        1.0 + viscosity * (axial_id**2 + mode_ids**2) + radial_eigen[None, None, :]
    )
    damping = damping.reshape(MTH, NR)
    place = jnp.stack([mine, row_index & 1, row_index >> 1, col_index >> 2, col_index & 3])
    lists = pair_lists(pair_list, owner_slot, place)
    terms = [window_terms(freq_list, snap_index[0] + t) for t in range(2)]
    weights = jnp.stack([terms[0][0], terms[0][1], terms[1][0], terms[1][1]], axis=1)
    weights = jnp.concatenate([weights, weights], axis=0)
    weights, damping = lax.optimization_barrier((weights, damping))

    out, keep, send = two_steps(lists, moved, synth, anal, stacked(analysis), stacked(synthesis), damping)

    back = lax.all_to_all(out, "col", split_axis=0, concat_axis=0, tiled=True)
    snaps = route(keep, send)
    retired = retire_old(block_dft, spectra)
    block, spectra_next = admit_new(weights, snaps, block_dft, retired)
    return (from_axial_major(back), block, spectra_next)


def solution(mesh):
    return jax.shard_map(
        local,
        mesh=mesh,
        in_specs=(
            P(None, "col", "row", None),
            P(),
            P(),
            P(),
            P(),
            P(),
            P(),
            P(),
            P(("row", "col"), None, None, None),
            P(("row", "col"), None, None, None, None),
        ),
        out_specs=(
            P(None, "col", "row", None),
            P(("row", "col"), None, None, None),
            P(("row", "col"), None, None, None, None),
        ),
        check_vma=False,
    )
```

time: 280 us -> 101 us (0.36)
  waiting for transfers between devices: 103 us -> 21.8 us
  matrix products: 72.4 us -> 0 us
  local copies, waits for them, and re-layouts: 39.7 us -> 0.52 us
  Pallas kernels: 0 us -> 38.1 us
  other arithmetic: 31.6 us -> 9.19 us
  between operations: 15.6 us -> 1.73 us
  starting transfers between devices: 14.4 us -> 28.2 us
    dot_general x10 -> x0, matrix products: 72.4 us -> none  [the longest x2 22 us: circle_forcing(): lax.dot_general(synth_table, columns, (((0,), (0,)), ((), ())), precision...]
    all_gather x1 -> x0, waiting for transfers between devices: 69.5 us -> none  [local(): gathered = lax.all_gather(compact, ('row', 'col'), axis=2, tiled=True)]
    pallas_call x0 -> x6, Pallas kernels: none -> 38.1 us  [the longest x1 18.1 us: two_steps(): pl.pallas_call(steps_kernel, out_shape=(pltpu.HBM((16, 64, NR), f32), plt...]
    mul x5 -> x1, other arithmetic: 29 us -> 0.01 us  [trig_tables(): 2 * lax.broadcasted_iota(jnp.int32, dims, mode_dim) + (kind & 1)]
    all_to_all x2, waiting for transfers between devices: 33.5 us -> 8.06 us  [the longest x1 8.06 us: local(): lax.all_to_all(to_axial_major(velocity), 'col', split_axis=0, concat_axis...]
    ppermute x0 -> x10, starting transfers between devices: none -> 16.7 us  [the longest x9 12.6 us: turn(): moved = lax.ppermute(blocks[k], axis, pairs_of(k))]
    ppermute x0 -> x10, waiting for transfers between devices: none -> 13.8 us  [the longest x9 13.8 us: turn(): moved = lax.ppermute(blocks[k], axis, pairs_of(k))]
    gather x6 -> x0, local copies, waits for them, and re-layouts: 13.3 us -> none  [the longest x1 3.74 us: local(): picked = both_snaps[:, :, mode_sel % modes_dev, axial_sel % axial_dev, :]]
  transfers between devices with their start and end apart: 3 -> 12, of which waited for: 2 -> 4; matrix products, arithmetic and copies ran while one was open for 14% -> 10% of each run, Pallas kernels for 0% -> 14%
where the time goes in v1:
time: 101 us; the launch traced here: 99.5 us
  Pallas kernels  38.1 us (38%)
  starting transfers between devices  28.2 us (28%)
  waiting for transfers between devices  21.8 us (22%)
  other arithmetic  9.19 us (9%)
  between operations  1.73 us (2%)
    pallas_call x1, Pallas kernels, two_steps(): pl.pallas_call(steps_kernel, out_shape=(pltpu.HBM((16, 64, NR), f32), plt...  18.1 us
    ppermute x9, waiting for transfers between devices, turn(): moved = lax.ppermute(blocks[k], axis, pairs_of(k))  13.8 us
    ppermute x9, starting transfers between devices, turn(): moved = lax.ppermute(blocks[k], axis, pairs_of(k))  12.6 us
    all_to_all x1, waiting for transfers between devices, local(): lax.all_to_all(to_axial_major(velocity), 'col', split_axis=0, concat_axis...  8.06 us
    all_to_all x1, starting transfers between devices, local(): lax.all_to_all(to_axial_major(velocity), 'col', split_axis=0, concat_axis...  7.7 us
    pallas_call x1, Pallas kernels, retire_old(): pl.pallas_call(retire_kernel, out_shape=jax.ShapeDtypeStruct((8, 2, NR, N...  7.48 us
    pallas_call x1, Pallas kernels, admit_new(): pl.pallas_call(admit_kernel, out_shape=(jax.ShapeDtypeStruct((8, 2, NR),...  4.74 us
    ppermute x1, starting transfers between devices, route(): got = lax.ppermute(send, 'row', [(i, i ^ 1) for i in range(8)])  4.1 us
  transfers between devices with their start and end apart: 12, of which 4 were waited for; matrix products, arithmetic and copies ran while one was open for 10% of the time, Pallas kernels for 14%

profile of v1, /device:TPU:1, one launch (start us, length us, event | category | flops | bytes accessed | tf_op | source)
XLA Modules:
  0.0 99.5 jit_solution(7235204618514507143)
XLA Ops:
  0.6 3.7 %axial_major.1 = f32[16,64,384]{2,1,0:T(8,128)} custom-call(f32[2,32,16,384]{3,2,1,0:T(8,128)} %src_ref.1), custom_call_target="tpu_custom_call" | custom-call | bytes 3145728 | tf_op jit(solution)/shard_map/axial_major/pallas_call | solution.py:69
  4.3 7.7 %all-to-all-start = ((f32[16,64,384]{2,1,0:T(8,128)}), f32[16,64,384]{2,1,0:T(8,128)S(1)}, u32[]{:S(2)}, u32[]{:S(2)}) async-start(f32[16,64,384]{2,1,0:T(8,128)} %axial_major.1), calls=%async_computation | async-start | bytes 3145728 | tf_op jit(solution)/shard_map/all_to_all | solution.py:489
  12.9 0.1 multiply_bitcast_fusion.3
  13.0 0.1 multiply_bitcast_fusion
  13.0 0.1 copy.16
  13.1 0.1 copy.13
  13.2 0.1 copy.14
  13.3 0.1 copy.15
  13.4 1.1 %add_divide_fusion.damp_any = f32[512,384]{1,0:T(8,128)} fusion(f32[384]{0:T(512)S(1)} %copy-done.6, f32[512]{0:T(512)S(1)} %multiply_add_fusion), kind=kLoop, calls=%fused_computation.32 | loop fusion | flops 393216 | bytes 790016 | tf_op jit(solution)/shard_map/div | solution.py:505
  14.5 0.1 maximum_maximum_fusion.weight_ref
  14.6 1.5 %reduce-precision_convert_fusion.1 = (bf16[4,384,256]{2,1,0:T(8,128)(2,1)S(1)}, bf16[4,384,256]{2,1,0:T(8,128)(2,1)S(1)}) fusion(f32[4]{0:T(128)S(1)} %compare_select_fusion.4, f32[384]{0:T(512)S(1)} %add_convert_fusion, s32[4]{0:T(128)S(1)} %iota_and_fusion, s32[256]{0:T(256)S(1)} %iota_multiply_fusion), kind=kLoop, calls=%fused_computation.5 | loop fusion | flops 11403264 | bytes 1575456 | tf_op jit(solution)/shard_map/convert_element_type | solution.py:58
  16.1 0.0 copy-start.1
  16.1 0.0 copy-start.2
  16.1 0.0 copy-start.4
  16.1 1.6 %pad_maximum_fusion.synth_any = bf16[4,384,768]{2,1,0:T(8,128)(2,1)} fusion(bf16[4,384,256]{2,1,0:T(8,128)(2,1)S(1)} %get-tuple-element.43, bf16[4,384,256]{2,1,0:T(8,128)(2,1)S(1)} %get-tuple-element.42), kind=kLoop, calls=%fused_computation | loop fusion | flops 7077888 | bytes 3932160 | tf_op jit(solution)/shard_map/concatenate | solution.py:492
  17.6 0.1 stack.38.place_ref
  17.7 2.2 %pair_lists.1 = (s32[1]{0:T(128)}, s32[257]{0:T(512)S(1)}, s32[257]{0:T(512)S(1)}) custom-call(s32[2,256]{1,0:T(2,128)S(1)} %bitcast.28, s32[256]{0:T(256)S(1)} %copy-done.2, s32[5]{0:T(128)S(1)} %stack.38.place_ref), custom_call_target="tpu_custom_call" | custom-call | bytes 8000000 | tf_op jit(solution)/shard_map/pair_lists/pallas_call | solution.py:131
  19.9 0.1 reduce-precision_convert_fusion.2
  20.0 0.1 reduce-precision_convert_fusion.3
  20.1 1.4 %pad_maximum_fusion.2 = (bf16[1152,384]{1,0:T(8,128)(2,1)}, bf16[1152,384]{1,0:T(8,128)(2,1)}) fusion(bf16[384,384]{1,0:T(8,128)(2,1)S(1)} %get-tuple-element.33, bf16[384,384]{1,0:T(8,128)(2,1)S(1)} %get-tuple-element.32, bf16[384,384]{1,0:T(8,128)(2,1)S(1)} %get-tuple-element.31, bf16[384,384]{1,0:T(8,128)(2,1)S(1)} %get-tuple-element.30), kind=kLoop, calls=%fused_computation.26 | loop fusion | flops 5308416 | bytes 2949120 | tf_op jit(solution)/shard_map/concatenate | solution.py:500
  21.5 1.6 %reduce-precision_convert_fusion = (bf16[4,256,384]{2,1,0:T(8,128)(2,1)S(1)}, bf16[4,256,384]{2,1,0:T(8,128)(2,1)S(1)}) fusion(f32[4]{0:T(128)S(1)} %compare_select_fusion.4, f32[384]{0:T(512)S(1)} %add_convert_fusion, s32[4]{0:T(128)S(1)} %iota_and_fusion, s32[256]{0:T(256)S(1)} %iota_multiply_fusion), kind=kLoop, calls=%fused_computation.3 | loop fusion | flops 11403264 | bytes 1575456 | tf_op jit(solution)/shard_map/convert_element_type | solution.py:58
  23.1 1.6 %pad_maximum_fusion.1.anal_any = bf16[4,256,1152]{2,1,0:T(8,128)(2,1)} fusion(bf16[4,256,384]{2,1,0:T(8,128)(2,1)S(1)} %get-tuple-element.41, bf16[4,256,384]{2,1,0:T(8,128)(2,1)S(1)} %get-tuple-element.40), kind=kLoop, calls=%fused_computation.1 | loop fusion | flops 7077888 | bytes 3932160 | tf_op jit(solution)/shard_map/concatenate | solution.py:494
  24.7 8.1 %all-to-all-done.moved_any = f32[16,64,384]{2,1,0:T(8,128)S(1)} async-done(((f32[16,64,384]{2,1,0:T(8,128)}), f32[16,64,384]{2,1,0:T(8,128)S(1)}, u32[]{:S(2)}, u32[]{:S(2)}) %all-to-all-start) | async-done | bytes 1572896 | tf_op jit(solution)/shard_map/all_to_all | solution.py:489
  32.8 18.1 %two_steps.1 = (f32[16,64,384]{2,1,0:T(8,128)}, f32[512,384]{1,0:T(8,128)}, f32[512,384]{1,0:T(8,128)}) custom-call(s32[1]{0:T(128)} %get-tuple-element.13.count_ref, s32[257]{0:T(512)S(1)} %get-tuple-element.14.spot_ref, s32[257]{0:T(512)S(1)} %get-tuple-element.15.mode_ref, f32[16,64,384]{2,1,0:T(8,128)S(1)} %all-to-all-done.moved_any, ...), custom_call_target="tpu_custom_call" | custom-call | flops 8000000000 | bytes 10000000 | tf_op jit(solution)/shard_map/two_steps/pallas_call | solution.py:306
  50.9 4.1 %collective-permute-start = (f32[512,384]{1,0:T(8,128)}, f32[512,384]{1,0:T(8,128)S(1)}, u32[]{:S(2)}, u32[]{:S(2)}) collective-permute-start(f32[512,384]{1,0:T(8,128)} %get-tuple-element.20), channel_id=1, source_target_pairs={{0,16},{16,0},{32,48},{48,32},{64,80},{80,64},{96,112},{112,96},{1... | collective-permute-start | bytes 2359304 | tf_op jit(solution)/shard_map/ppermute | solution.py:455
  55.0 3.8 %all-to-all-start.1 = ((f32[16,64,384]{2,1,0:T(8,128)}), f32[16,64,384]{2,1,0:T(8,128)S(1)}, u32[]{:S(2)}, u32[]{:S(2)}) async-start(f32[16,64,384]{2,1,0:T(8,128)} %get-tuple-element.17), calls=%async_computation.1 | async-start | bytes 3145728 | tf_op jit(solution)/shard_map/all_to_all | solution.py:518
  58.8 0.0 copy-start
  58.8 0.1 slice_add_fusion.2
  58.9 1.7 %collective-permute-start.1 = (f32[128,384]{1,0:T(8,128)S(1)}, f32[128,384]{1,0:T(8,128)S(1)}, u32[]{:S(2)}, u32[]{:S(2)}) collective-permute-start(f32[128,384]{1,0:T(8,128)S(1)} %get-tuple-element.27), channel_id=1, source_target_pairs={{0,32},{16,48},{32,64},{48,80},{64,96},{80,112},{96,0},{112,16},{1... | collective-permute-start | bytes 589832 | tf_op jit(solution)/shard_map/ppermute | solution.py:462
  60.6 2.2 %collective-permute-start.3 = (f32[128,384]{1,0:T(8,128)S(1)}, f32[128,384]{1,0:T(8,128)S(1)}, u32[]{:S(2)}, u32[]{:S(2)}) collective-permute-start(f32[128,384]{1,0:T(8,128)S(1)} %get-tuple-element.28), channel_id=1, source_target_pairs={{0,96},{16,112},{32,0},{48,16},{64,32},{80,48},{96,64},{112,80},{1... | collective-permute-start | bytes 589832 | tf_op jit(solution)/shard_map/ppermute | solution.py:462
  62.8 1.2 %collective-permute-start.2 = (f32[128,384]{1,0:T(8,128)S(1)}, f32[128,384]{1,0:T(8,128)S(1)}, u32[]{:S(2)}, u32[]{:S(2)}) collective-permute-start(f32[128,384]{1,0:T(8,128)S(1)} %get-tuple-element.29), channel_id=1, source_target_pairs={{0,64},{16,80},{32,96},{48,112},{64,0},{80,16},{96,32},{112,48},{1... | collective-permute-start | bytes 589832 | tf_op jit(solution)/shard_map/ppermute | solution.py:462
  64.0 3.8 %collective-permute-done.1 = f32[128,384]{1,0:T(8,128)S(1)} collective-permute-done((f32[128,384]{1,0:T(8,128)S(1)}, f32[128,384]{1,0:T(8,128)S(1)}, u32[]{:S(2)}, u32[]{:S(2)}) %collective-permute-start.1) | collective-permute-done | bytes 196640 | tf_op jit(solution)/shard_map/ppermute | solution.py:462
  67.8 0.0 collective-permute-done.3
  67.8 5.1 %collective-permute-done.2 = f32[128,384]{1,0:T(8,128)S(1)} collective-permute-done((f32[128,384]{1,0:T(8,128)S(1)}, f32[128,384]{1,0:T(8,128)S(1)}, u32[]{:S(2)}, u32[]{:S(2)}) %collective-permute-start.2) | collective-permute-done | bytes 196640 | tf_op jit(solution)/shard_map/ppermute | solution.py:462
  73.0 1.0 collective-permute-start.4
  73.9 1.8 %collective-permute-start.6 = (f32[32,384]{1,0:T(8,128)S(1)}, f32[32,384]{1,0:T(8,128)S(1)}, u32[]{:S(2)}, u32[]{:S(2)}) collective-permute-start(f32[32,384]{1,0:T(8,128)S(1)} %get-tuple-element.35), channel_id=1, source_target_pairs={{0,12},{1,13},{2,14},{3,15},{4,0},{5,1},{6,2},{7,3},{8,4},{9,5},{1... | collective-permute-start | bytes 147464 | tf_op jit(solution)/shard_map/ppermute | solution.py:462
  75.7 1.2 %collective-permute-start.5 = (f32[32,384]{1,0:T(8,128)S(1)}, f32[32,384]{1,0:T(8,128)S(1)}, u32[]{:S(2)}, u32[]{:S(2)}) collective-permute-start(f32[32,384]{1,0:T(8,128)S(1)} %get-tuple-element.36), channel_id=1, source_target_pairs={{0,8},{1,9},{2,10},{3,11},{4,12},{5,13},{6,14},{7,15},{8,0},{9,1},... | collective-permute-start | bytes 147464 | tf_op jit(solution)/shard_map/ppermute | solution.py:462
  76.9 4.9 %collective-permute-done.4 = f32[32,384]{1,0:T(8,128)S(1)} collective-permute-done((f32[32,384]{1,0:T(8,128)S(1)}, f32[32,384]{1,0:T(8,128)S(1)}, u32[]{:S(2)}, u32[]{:S(2)}) %collective-permute-start.4) | collective-permute-done | bytes 49184 | tf_op jit(solution)/shard_map/ppermute | solution.py:462
  81.8 0.0 collective-permute-done.6
  81.8 0.0 collective-permute-done.5
  81.9 1.1 %collective-permute-start.7 = (f32[8,384]{1,0:T(8,128)S(1)}, f32[8,384]{1,0:T(8,128)S(1)}, u32[]{:S(2)}, u32[]{:S(2)}) collective-permute-start(f32[8,384]{1,0:T(8,128)S(1)} %get-tuple-element.37), channel_id=1, source_target_pairs={{0,1},{1,2},{2,3},{3,0},{4,5},{5,6},{6,7},{7,4},{8,9},{9,10},{10,1... | collective-permute-start | bytes 36872 | tf_op jit(solution)/shard_map/ppermute | solution.py:462
  83.0 1.6 %collective-permute-start.9 = (f32[8,384]{1,0:T(8,128)S(1)}, f32[8,384]{1,0:T(8,128)S(1)}, u32[]{:S(2)}, u32[]{:S(2)}) collective-permute-start(f32[8,384]{1,0:T(8,128)S(1)} %get-tuple-element.38), channel_id=1, source_target_pairs={{0,3},{1,0},{2,1},{3,2},{4,7},{5,4},{6,5},{7,6},{8,11},{9,8},{10,9... | collective-permute-start | bytes 36872 | tf_op jit(solution)/shard_map/ppermute | solution.py:462
  84.6 0.7 collective-permute-start.8
  85.4 7.5 %retire_old.1.retired_ref = f32[8,2,384,384]{3,2,1,0:T(8,128)S(1)} custom-call(f32[8,2,384]{2,1,0:T(2,128)S(1)} %bitcast.26, f32[8,2,384,384]{3,2,1,0:T(8,128)} %bitcast.29), custom_call_target="tpu_custom_call" | custom-call | flops 300000000 | bytes 19000000 | tf_op jit(solution)/shard_map/retire_old/pallas_call | solution.py:367
  92.8 0.0 collective-permute-done.7
  92.9 0.0 collective-permute-done.9
  92.9 4.7 %admit_new.1 = (f32[8,2,384]{2,1,0:T(2,128)}, f32[8,2,384,384]{3,2,1,0:T(8,128)}) custom-call(f32[8,4]{1,0:T(8,128)S(1)} %maximum_maximum_fusion.weight_ref, f32[8,384]{1,0:T(8,128)S(1)} %fusion.18.snap_ref, f32[8,2,384]{2,1,0:T(2,128)S(1)} %bitcast.27, f32[8,2,384,384]{3,2,1,0:T(8,128)S(1)} %retire_old.1.retired_ref), custom_call_target="tpu_custom_call" | custom-call | flops 300000000 | bytes 10000000 | tf_op jit(solution)/shard_map/admit_new/pallas_call | solution.py:430
  97.7 1.9 %mode_major.1 = f32[2,32,16,384]{3,2,1,0:T(8,128)} custom-call(f32[16,64,384]{2,1,0:T(8,128)S(1)} %all-to-all-done.1.src_ref), custom_call_target="tpu_custom_call" | custom-call | bytes 3145728 | tf_op jit(solution)/shard_map/mode_major/pallas_call | solution.py:90
  (28 shorter events, 0.2 us)
Async XLA Ops:
  4.3 8.6 %copy-start.7 = (s32[4]{0:T(128)S(1)}, s32[4]{0:T(128)}, u32[]{:S(2)}) copy-start(s32[4]{0:T(128)} %param.16) | copy-start | bytes 52
  4.3 9.1 %copy-start.6 = (f32[384]{0:T(512)S(1)}, f32[384]{0:T(512)}, u32[]{:S(2)}) copy-start(f32[384]{0:T(512)} %param.13) | copy-start | bytes 4612
  4.3 28.4 %all-to-all-start = ((f32[16,64,384]{2,1,0:T(8,128)}), f32[16,64,384]{2,1,0:T(8,128)S(1)}, u32[]{:S(2)}, u32[]{:S(2)}) async-start(f32[16,64,384]{2,1,0:T(8,128)} %axial_major.1), calls=%async_computation | async-start | bytes 3145728 | tf_op jit(solution)/shard_map/all_to_all | solution.py:489
  16.1 1.7 %copy-start.1 = (s32[256,2]{0,1:T(2,128)S(1)}, s32[256,2]{0,1:T(2,128)}, u32[]{:S(2)}) copy-start(s32[256,2]{0,1:T(2,128)} %param.14) | copy-start | bytes 6148
  16.1 1.7 %copy-start.2 = (s32[256]{0:T(256)S(1)}, s32[256]{0:T(256)}, u32[]{:S(2)}) copy-start(s32[256]{0:T(256)} %owner_ref.1) | copy-start | bytes 3076
  16.1 3.9 %copy-start.4 = (f32[384,384]{1,0:T(8,128)S(1)}, f32[384,384]{1,0:T(8,128)}, u32[]{:S(2)}) copy-start(f32[384,384]{1,0:T(8,128)} %param.11) | copy-start | bytes 1769476
  17.6 2.4 %copy-start.5 = (f32[384,384]{1,0:T(8,128)S(1)}, f32[384,384]{1,0:T(8,128)}, u32[]{:S(2)}) copy-start(f32[384,384]{1,0:T(8,128)} %param.12) | copy-start | bytes 1769476
  50.9 8.0 %collective-permute-start = (f32[512,384]{1,0:T(8,128)}, f32[512,384]{1,0:T(8,128)S(1)}, u32[]{:S(2)}, u32[]{:S(2)}) collective-permute-start(f32[512,384]{1,0:T(8,128)} %get-tuple-element.20), channel_id=1, source_target_pairs={{0,16},{16,0},{32,48},{48,32},{64,80},{80,64},{96,112},{112,96},{1... | collective-permute-start | bytes 2359304 | tf_op jit(solution)/shard_map/ppermute | solution.py:455
  55.0 3.9 %copy-start.3 = (f32[512,384]{1,0:T(8,128)S(1)}, f32[512,384]{1,0:T(8,128)}, u32[]{:S(2)}) copy-start(f32[512,384]{1,0:T(8,128)} %get-tuple-element.19) | copy-start | bytes 2359300
  55.0 42.7 %all-to-all-start.1 = ((f32[16,64,384]{2,1,0:T(8,128)}), f32[16,64,384]{2,1,0:T(8,128)S(1)}, u32[]{:S(2)}, u32[]{:S(2)}) async-start(f32[16,64,384]{2,1,0:T(8,128)} %get-tuple-element.17), calls=%async_computation.1 | async-start | bytes 3145728 | tf_op jit(solution)/shard_map/all_to_all | solution.py:518
  58.8 26.5 %copy-start = (f32[2,4,2,384]{3,2,1,0:T(2,128)S(1)}, f32[2,4,2,384]{3,2,1,0:T(2,128)}, u32[]{:S(2)}) copy-start(f32[2,4,2,384]{3,2,1,0:T(2,128)} %param.18) | copy-start | bytes 73732
  58.9 8.9 %collective-permute-start.1 = (f32[128,384]{1,0:T(8,128)S(1)}, f32[128,384]{1,0:T(8,128)S(1)}, u32[]{:S(2)}, u32[]{:S(2)}) collective-permute-start(f32[128,384]{1,0:T(8,128)S(1)} %get-tuple-element.27), channel_id=1, source_target_pairs={{0,32},{16,48},{32,64},{48,80},{64,96},{80,112},{96,0},{112,16},{1... | collective-permute-start | bytes 589832 | tf_op jit(solution)/shard_map/ppermute | solution.py:462
  60.6 7.2 %collective-permute-start.3 = (f32[128,384]{1,0:T(8,128)S(1)}, f32[128,384]{1,0:T(8,128)S(1)}, u32[]{:S(2)}, u32[]{:S(2)}) collective-permute-start(f32[128,384]{1,0:T(8,128)S(1)} %get-tuple-element.28), channel_id=1, source_target_pairs={{0,96},{16,112},{32,0},{48,16},{64,32},{80,48},{96,64},{112,80},{1... | collective-permute-start | bytes 589832 | tf_op jit(solution)/shard_map/ppermute | solution.py:462
  62.8 10.1 %collective-permute-start.2 = (f32[128,384]{1,0:T(8,128)S(1)}, f32[128,384]{1,0:T(8,128)S(1)}, u32[]{:S(2)}, u32[]{:S(2)}) collective-permute-start(f32[128,384]{1,0:T(8,128)S(1)} %get-tuple-element.29), channel_id=1, source_target_pairs={{0,64},{16,80},{32,96},{48,112},{64,0},{80,16},{96,32},{112,48},{1... | collective-permute-start | bytes 589832 | tf_op jit(solution)/shard_map/ppermute | solution.py:462
  73.0 8.9 %collective-permute-start.4 = (f32[32,384]{1,0:T(8,128)S(1)}, f32[32,384]{1,0:T(8,128)S(1)}, u32[]{:S(2)}, u32[]{:S(2)}) collective-permute-start(f32[32,384]{1,0:T(8,128)S(1)} %get-tuple-element.34), channel_id=1, source_target_pairs={{0,4},{1,5},{2,6},{3,7},{4,8},{5,9},{6,10},{7,11},{8,12},{9,13},{1... | collective-permute-start | bytes 147464 | tf_op jit(solution)/shard_map/ppermute | solution.py:462
  73.9 7.9 %collective-permute-start.6 = (f32[32,384]{1,0:T(8,128)S(1)}, f32[32,384]{1,0:T(8,128)S(1)}, u32[]{:S(2)}, u32[]{:S(2)}) collective-permute-start(f32[32,384]{1,0:T(8,128)S(1)} %get-tuple-element.35), channel_id=1, source_target_pairs={{0,12},{1,13},{2,14},{3,15},{4,0},{5,1},{6,2},{7,3},{8,4},{9,5},{1... | collective-permute-start | bytes 147464 | tf_op jit(solution)/shard_map/ppermute | solution.py:462
  75.7 6.1 %collective-permute-start.5 = (f32[32,384]{1,0:T(8,128)S(1)}, f32[32,384]{1,0:T(8,128)S(1)}, u32[]{:S(2)}, u32[]{:S(2)}) collective-permute-start(f32[32,384]{1,0:T(8,128)S(1)} %get-tuple-element.36), channel_id=1, source_target_pairs={{0,8},{1,9},{2,10},{3,11},{4,12},{5,13},{6,14},{7,15},{8,0},{9,1},... | collective-permute-start | bytes 147464 | tf_op jit(solution)/shard_map/ppermute | solution.py:462
  81.9 11.0 %collective-permute-start.7 = (f32[8,384]{1,0:T(8,128)S(1)}, f32[8,384]{1,0:T(8,128)S(1)}, u32[]{:S(2)}, u32[]{:S(2)}) collective-permute-start(f32[8,384]{1,0:T(8,128)S(1)} %get-tuple-element.37), channel_id=1, source_target_pairs={{0,1},{1,2},{2,3},{3,0},{4,5},{5,6},{6,7},{7,4},{8,9},{9,10},{10,1... | collective-permute-start | bytes 36872 | tf_op jit(solution)/shard_map/ppermute | solution.py:462
  83.0 9.9 %collective-permute-start.9 = (f32[8,384]{1,0:T(8,128)S(1)}, f32[8,384]{1,0:T(8,128)S(1)}, u32[]{:S(2)}, u32[]{:S(2)}) collective-permute-start(f32[8,384]{1,0:T(8,128)S(1)} %get-tuple-element.38), channel_id=1, source_target_pairs={{0,3},{1,0},{2,1},{3,2},{4,7},{5,4},{6,5},{7,6},{8,11},{9,8},{10,9... | collective-permute-start | bytes 36872 | tf_op jit(solution)/shard_map/ppermute | solution.py:462
  84.6 8.2 %collective-permute-start.8 = (f32[8,384]{1,0:T(8,128)S(1)}, f32[8,384]{1,0:T(8,128)S(1)}, u32[]{:S(2)}, u32[]{:S(2)}) collective-permute-start(f32[8,384]{1,0:T(8,128)S(1)} %get-tuple-element.39), channel_id=1, source_target_pairs={{0,2},{1,3},{2,0},{3,1},{4,6},{5,7},{6,4},{7,5},{8,10},{9,11},{10,... | collective-permute-start | bytes 36872 | tf_op jit(solution)/shard_map/ppermute | solution.py:462

commit v2 on v1

--- a/solution.py
+++ b/solution.py
@@ -59,40 +59,79 @@
     return high, low
 
 
-def gather_kernel(src_ref, out_ref):
-    for parity in range(2):
-        block = jnp.stack([src_ref[0, 2 * i + parity] for i in range(8)])
-        out_ref[:, parity * 8 : parity * 8 + 8, :] = pltpu.einshape("mar->amr", block)
+def gather_kernel(src_any, out_any, src, out, sems):
+    blocks = [(c, half) for c in range(2) for half in range(2)]
+    reads = [
+        pltpu.make_async_copy(
+            src_any.at[c, pl.ds(half * 16 + 8 * q, 8)], src.at[c, pl.ds(half * 16 + 8 * q, 8)], sems.at[4 * c + 2 * half + q]
+        )
+        for c, half in blocks
+        for q in range(2)
+    ]
+    for copy in reads:
+        copy.start()
+    writes = []
+    for n, (c, half) in enumerate(blocks):
+        reads[2 * n].wait()
+        reads[2 * n + 1].wait()
+        for parity in range(2):
+            block = jnp.stack([src[c, half * 16 + 2 * i + parity] for i in range(8)])
+            row = n * 16 + parity * 8
+            out[:, row : row + 8, :] = pltpu.einshape("mar->amr", block)
+            at = pl.ds(row, 8)
+            for q in range(2):
+                these = pl.ds(8 * q, 8)
+                writes.append(
+                    pltpu.make_async_copy(
+                        out.at[these, at], out_any.at[these, at], sems.at[8 + 4 * n + 2 * parity + q]
+                    )
+                )
+                writes[-1].start()
+    for copy in writes:
+        copy.wait()
 
 
 def to_axial_major(velocity):
     return pl.pallas_call(
         gather_kernel,
-        out_shape=jax.ShapeDtypeStruct((16, 64, NR), f32),
-        grid=(2, 2),
-        in_specs=[pl.BlockSpec((1, 16, 16, NR), lambda c, i: (c, i, 0, 0))],
-        out_specs=pl.BlockSpec((16, 16, NR), lambda c, i: (0, 2 * c + i, 0)),
+        out_shape=pltpu.HBM((16, 64, NR), f32),
+        in_specs=[HBM],
+        out_specs=HBM,
+        scratch_shapes=[
+            pltpu.VMEM((2, 32, 16, NR), f32),
+            pltpu.VMEM((16, 64, NR), f32),
+            pltpu.SemaphoreType.DMA((24,)),
+        ],
         compiler_params=params(8),
         cost_estimate=pl.CostEstimate(flops=0, bytes_accessed=2 * 1024 * NR * 4, transcendentals=0),
         name="axial_major",
     )(in_hbm(velocity))
 
 
-def scatter_kernel(src_ref, out_ref):
-    for parity in range(2):
-        block = src_ref[:, parity * 8 : parity * 8 + 8, :]
-        moved = pltpu.einshape("amr->mar", block)
-        for i in range(8):
-            out_ref[0, 2 * i + parity] = moved[i]
+def scatter_kernel(src, out_any, out, sems):
+    writes = []
+    for n in range(4):
+        c, half = n // 2, n % 2
+        for parity in range(2):
+            row = n * 16 + parity * 8
+            moved = pltpu.einshape("amr->mar", src[:, row : row + 8, :])
+            for i in range(8):
+                out[c, half * 16 + 2 * i + parity] = moved[i]
+        for q in range(2):
+            at = pl.ds(half * 16 + 8 * q, 8)
+            writes.append(pltpu.make_async_copy(out.at[c, at], out_any.at[c, at], sems.at[2 * n + q]))
+            writes[-1].start()
+    for copy in writes:
+        copy.wait()
 
 
 def from_axial_major(moved):
     return pl.pallas_call(
         scatter_kernel,
         out_shape=jax.ShapeDtypeStruct((2, 32, 16, NR), f32),
-        grid=(2, 2),
-        in_specs=[pl.BlockSpec((16, 16, NR), lambda c, i: (0, 2 * c + i, 0))],
-        out_specs=pl.BlockSpec((1, 16, 16, NR), lambda c, i: (c, i, 0, 0)),
+        in_specs=[VMEM],
+        out_specs=ANY,
+        scratch_shapes=[pltpu.VMEM((2, 32, 16, NR), f32), pltpu.SemaphoreType.DMA((8,))],
         compiler_params=params(8),
         cost_estimate=pl.CostEstimate(flops=0, bytes_accessed=2 * 1024 * NR * 4, transcendentals=0),
         name="mode_major",
@@ -148,7 +187,8 @@
     return high, (value - high.astype(f32)).astype(bf16)
 
 
-BANDS = ((0, 256), (256, 128))
+WIDE = 256
+REST = NR - WIDE
 
 
 def steps_kernel(
@@ -171,8 +211,10 @@
     synthesis_ref,
     damp_ref,
     cols,
+    cols_rest,
     phys,
     squares,
+    squares_rest,
     rows,
     parcel,
     sems,
@@ -189,6 +231,11 @@
             for half in range(2)
         ]
         for part in range(4)
+    ]
+    field_out = [
+        pltpu.make_async_copy(held(part, half), strip(out_any, part, half), sems.at[2 * part + half])
+        for part in range(4)
+        for half in range(2)
     ]
     synth_in = [
         pltpu.make_async_copy(synth_any.at[part], synth_ref.at[part], sems.at[8 + part]) for part in range(4)
@@ -207,42 +254,53 @@
         copy.start()
     parcel[...] = jnp.zeros_like(parcel)
 
-    def store_rows(at, lanes, value):
+    def store_rows(at, start, value):
         high, low = split(value)
-        start, width = lanes
+        width = value.shape[1]
         rows[at, start : start + width] = high
         rows[at, NR + start : NR + start + width] = low
-        rows[at, 2 * NR + start : 2 * NR + start + width] = high
-
-    def step(t, carry):
-        for start, width in BANDS:
+
+    def store_stack(wide, rest, part, size, b, count, band, value):
+        high, low = split(value)
+        if band == 0:
+            wide[part, pl.ds(b, count), :] = high
+            wide[part, pl.ds(size + b, count), :] = low
+            wide[part, pl.ds(2 * size + b, count), :] = high
+        else:
+            rest[part, pl.ds(b, count), 0:REST] = high
+            rest[part, pl.ds(b, count), REST : 2 * REST] = low
+
+    def against(table, wide, rest, part, size, band):
+        if band == 0:
+            return jnp.dot(table[part], wide[part], preferred_element_type=f32)
+        both = jnp.dot(table[part, :, 0:size], rest[part], preferred_element_type=f32)
+        low = jnp.dot(table[part, :, 2 * size : 3 * size], rest[part, :, 0:REST], preferred_element_type=f32)
+        return both[:, 0:REST] + both[:, REST:] + low
+
+    def solve(at, matrix, then):
+        both = jnp.dot(rows[at, :], matrix[:, 0 : WIDE + 2 * REST], preferred_element_type=f32)
+        low = jnp.dot(rows[at, 0:NR], matrix[0:NR, WIDE + 2 * REST :], preferred_element_type=f32)
+        then(0, both[:, 0:WIDE] + low)
+        then(WIDE, both[:, WIDE:NR] + both[:, NR:])
+
+    bands = ((0, WIDE), (WIDE, REST))
+
+    def step(t):
+        for band, (start, width) in enumerate(bands):
             lanes = pl.ds(start, width)
             for part in range(4):
-                if start == 0:
-
-                    @pl.when(t == 0)
-                    def _():
-                        for copy in moved_in[part]:
-                            copy.wait()
-                        synth_in[part].wait()
-
                 for b in range(0, HALF, 64):
                     scaled = state[part, pl.ds(b // 16, 4), :, lanes].reshape(64, width) * SYNTH_WEIGHT
                     if part == 0 and b == 0:
                         first_row = lax.broadcasted_iota(jnp.int32, scaled.shape, 0) == 0
                         scaled = jnp.where(first_row, 0.5 * scaled, scaled)
-                    high, low = split(scaled)
-                    cols[part, pl.ds(b, 64), lanes] = high
-                    cols[part, pl.ds(HALF + b, 64), lanes] = low
-                    cols[part, pl.ds(2 * HALF + b, 64), lanes] = high
-                phys[part, :, lanes] = jnp.dot(synth_ref[part], cols[part, :, lanes], preferred_element_type=f32)
-
-        @pl.when(t == 0)
-        def _():
+                    store_stack(cols, cols_rest, part, HALF, b, 64, band, scaled)
+                phys[part, :, lanes] = against(synth_ref, cols, cols_rest, part, HALF, band)
+
+        if t == 0:
             for copy in anal_in + rest_in:
                 copy.wait()
-
-        for start, width in BANDS:
+        for band, (start, width) in enumerate(bands):
             lanes = pl.ds(start, width)
             for b in range(0, QUARTER, 32):
                 ce, co, se, so = (phys[part, pl.ds(b, 32), lanes] for part in range(4))
@@ -250,27 +308,33 @@
                 near, far = a * a + s * s, b_ * b_ + d * d
                 near_x, far_x = a * s, b_ * d
                 for part, value in enumerate((near + far, near - far, near_x + far_x, near_x - far_x)):
-                    high, low = split(value)
-                    squares[part, pl.ds(b, 32), lanes] = high
-                    squares[part, pl.ds(QUARTER + b, 32), lanes] = low
-                    squares[part, pl.ds(2 * QUARTER + b, 32), lanes] = high
+                    store_stack(squares, squares_rest, part, QUARTER, b, 32, band, value)
             for part in range(4):
-                folded = jnp.dot(anal_ref[part], squares[part, :, lanes], preferred_element_type=f32)
+                folded = against(anal_ref, squares, squares_rest, part, QUARTER, band)
                 gain = -nonlinear_gain * KEEP * (2.0 if part < 2 else 4.0)
                 if part == 0:
                     first_row = lax.broadcasted_iota(jnp.int32, folded.shape, 0) == 0
                     folded = jnp.where(first_row, 0.0, folded)
                 old = state[part, :, :, lanes].reshape(HALF, width)
-                store_rows(pl.ds(part * HALF, HALF), (start, width), old + gain * folded)
+                store_rows(pl.ds(part * HALF, HALF), start, old + gain * folded)
         for half in range(2):
             at = pl.ds(half * MTH, MTH)
-            coeffs = jnp.dot(rows[at, :], analysis_ref[...], preferred_element_type=f32)
-            store_rows(at, (0, NR), coeffs * damp_ref[...])
+
+            def damped(start, value):
+                store_rows(at, start, value * damp_ref[:, start : start + value.shape[1]])
+
+            solve(at, analysis_ref, damped)
         for half in range(2):
-            at = pl.ds(half * MTH, MTH)
-            value = jnp.dot(rows[at, :], synthesis_ref[...], preferred_element_type=f32)
-            state[pl.ds(2 * half, 2)] = value.reshape(2, 16, 16, NR)
-        return carry
+
+            def placed(start, value):
+                width = value.shape[1]
+                state[pl.ds(2 * half, 2), :, :, start : start + width] = value.reshape(2, 16, 16, width)
+
+            solve(pl.ds(half * MTH, MTH), synthesis_ref, placed)
+
+            if t == 1:
+                for copy in field_out[4 * half : 4 * half + 4]:
+                    copy.start()
 
     def pick(t):
         def one(i, carry):
@@ -283,22 +347,19 @@
 
         lax.fori_loop(0, count_ref[0], one, 0)
 
-    def step_and_pick(t, carry):
-        step(t, 0)
+    for part in range(4):
+        for copy in moved_in[part] + [synth_in[part]]:
+            copy.wait()
+    for t in range(2):
+        step(t)
         pick(t)
-        return carry
-
-    lax.fori_loop(0, 2, step_and_pick, 0)
-    copies = [
-        pltpu.make_async_copy(held(part, half), strip(out_any, part, half), sems.at[2 * part + half])
-        for part in range(4)
-        for half in range(2)
+    parcel_out = [
+        pltpu.make_async_copy(parcel.at[pl.ds(512, 512)], send_any, sems.at[8]),
+        pltpu.make_async_copy(parcel.at[pl.ds(0, 512)], keep_any, sems.at[9]),
     ]
-    copies.append(pltpu.make_async_copy(parcel.at[pl.ds(512, 512)], send_any, sems.at[8]))
-    copies.append(pltpu.make_async_copy(parcel.at[pl.ds(0, 512)], keep_any, sems.at[9]))
-    for copy in copies:
+    for copy in parcel_out:
         copy.start()
-    for copy in copies:
+    for copy in field_out + parcel_out:
         copy.wait()
 
 
@@ -316,13 +377,15 @@
             pltpu.VMEM((4, 16, 16, NR), f32),
             pltpu.VMEM((4, QUARTER, 3 * HALF), bf16),
             pltpu.VMEM((4, HALF, 3 * QUARTER), bf16),
-            pltpu.VMEM((3 * NR, NR), bf16),
-            pltpu.VMEM((3 * NR, NR), bf16),
+            pltpu.VMEM((2 * NR, 2 * NR), bf16),
+            pltpu.VMEM((2 * NR, 2 * NR), bf16),
             pltpu.VMEM((MTH, NR), f32),
-            pltpu.VMEM((4, 3 * HALF, NR), bf16),
+            pltpu.VMEM((4, 3 * HALF, WIDE), bf16),
+            pltpu.VMEM((4, HALF, 2 * REST), bf16),
             pltpu.VMEM((4, QUARTER, NR), f32),
-            pltpu.VMEM((4, 3 * QUARTER, NR), bf16),
-            pltpu.VMEM((1024, 3 * NR), bf16),
+            pltpu.VMEM((4, 3 * QUARTER, WIDE), bf16),
+            pltpu.VMEM((4, QUARTER, 2 * REST), bf16),
+            pltpu.VMEM((1024, 2 * NR), bf16),
             pltpu.VMEM((1024, NR), f32),
             pltpu.SemaphoreType.DMA((19,)),
         ],
@@ -467,8 +530,7 @@
     blocks = [total[k * 32 : (k + 1) * 32] for k in range(4)]
     total = turn(blocks, "col", lambda k: [(x * 4 + y, (x + k) % 4 * 4 + y) for x in range(4) for y in range(4)])
     blocks = [total[k * 8 : (k + 1) * 8] for k in range(4)]
-    snaps = turn(blocks, "col", lambda k: [(x * 4 + y, x * 4 + (y + k) % 4) for x in range(4) for y in range(4)])
-    return snaps
+    return turn(blocks, "col", lambda k: [(x * 4 + y, x * 4 + (y + k) % 4) for x in range(4) for y in range(4)])
 
 
 def local(
@@ -497,7 +559,9 @@
         high = lax.reduce_precision(matrix, 8, 7)
         low = matrix - high
         high, low = high.astype(bf16), low.astype(bf16)
-        return jnp.concatenate([high, high, low], axis=0)
+        upper = jnp.concatenate([high, low[:, WIDE:], low[:, :WIDE]], axis=1)
+        lower = jnp.concatenate([high, jnp.zeros((NR, NR), bf16)], axis=1)
+        return jnp.concatenate([upper, lower], axis=0)
 
     parity = jnp.arange(2, dtype=jnp.int32)[:, None, None]
     mode_ids = (2 * jnp.arange(HALF, dtype=jnp.int32)[None, :, None] + parity).astype(f32)

time: 101 us -> 96.7 us (0.957)
  Pallas kernels: 38.1 us -> 33.2 us
  waiting for transfers between devices: 21.8 us -> 20.7 us
    pallas_call x1, Pallas kernels: 18.1 us -> 15 us  [two_steps(): pl.pallas_call(steps_kernel, out_shape=(pltpu.HBM((16, 64, NR), f32), plt...]
    pallas_call x1, Pallas kernels: 3.67 us -> 2.46 us  [to_axial_major(): pl.pallas_call(gather_kernel, out_shape=pltpu.HBM((16, 64, NR), f32), in_...]
    all_to_all x1, waiting for transfers between devices: 8.06 us -> 6.87 us  [local(): lax.all_to_all(to_axial_major(velocity), 'col', split_axis=0, concat_axis...]
  transfers between devices with their start and end apart: 12 -> 12, of which waited for: 4 -> 4; matrix products, arithmetic and copies ran while one was open for 10% -> 11% of each run, Pallas kernels for 14% -> 15%
where the time goes in v2:
time: 96.7 us; the launch traced here: 94.9 us
  Pallas kernels  33.2 us (34%)
  starting transfers between devices  28.2 us (29%)
  waiting for transfers between devices  20.7 us (21%)
  other arithmetic  9.47 us (10%)
  between operations  1.94 us (2%)
  local copies, waits for them, and re-layouts  1.38 us (1%)
    pallas_call x1, Pallas kernels, two_steps(): pl.pallas_call(steps_kernel, out_shape=(pltpu.HBM((16, 64, NR), f32), plt...  15 us
    ppermute x9, waiting for transfers between devices, turn(): moved = lax.ppermute(blocks[k], axis, pairs_of(k))  13.8 us
    ppermute x9, starting transfers between devices, turn(): moved = lax.ppermute(blocks[k], axis, pairs_of(k))  12.6 us
    all_to_all x1, starting transfers between devices, local(): lax.all_to_all(to_axial_major(velocity), 'col', split_axis=0, concat_axis...  7.72 us
    pallas_call x1, Pallas kernels, retire_old(): pl.pallas_call(retire_kernel, out_shape=jax.ShapeDtypeStruct((8, 2, NR, N...  7.48 us
    all_to_all x1, waiting for transfers between devices, local(): lax.all_to_all(to_axial_major(velocity), 'col', split_axis=0, concat_axis...  6.87 us
    pallas_call x1, Pallas kernels, admit_new(): pl.pallas_call(admit_kernel, out_shape=(jax.ShapeDtypeStruct((8, 2, NR),...  4.74 us
    ppermute x1, starting transfers between devices, route(): got = lax.ppermute(send, 'row', [(i, i ^ 1) for i in range(8)])  4.1 us
  transfers between devices with their start and end apart: 12, of which 4 were waited for; matrix products, arithmetic and copies ran while one was open for 11% of the time, Pallas kernels for 15%

profile of v2, /device:TPU:1, one launch (start us, length us, event | category | flops | bytes accessed | tf_op | source)
XLA Modules:
  0.0 94.9 jit_solution(1441234072035220926)
XLA Ops:
  0.6 2.5 %axial_major.1 = f32[16,64,384]{2,1,0:T(8,128)} custom-call(f32[2,32,16,384]{3,2,1,0:T(8,128)} %src_any.1), custom_call_target="tpu_custom_call" | custom-call | bytes 3145728 | tf_op jit(solution)/shard_map/axial_major/pallas_call | solution.py:95
  3.1 0.0 copy-start.4
  3.1 7.7 %all-to-all-start = ((f32[16,64,384]{2,1,0:T(8,128)}), f32[16,64,384]{2,1,0:T(8,128)S(1)}, u32[]{:S(2)}, u32[]{:S(2)}) async-start(f32[16,64,384]{2,1,0:T(8,128)} %axial_major.1), calls=%async_computation | async-start | bytes 3145728 | tf_op jit(solution)/shard_map/all_to_all | solution.py:551
  10.8 0.0 copy-start.5
  10.9 0.0 copy-start.7
  10.9 0.0 copy-start.6
  10.9 0.1 fusion.15
  11.0 0.0 copy-start.1
  11.1 0.0 copy-start.2
  11.1 0.8 copy-done.5
  11.9 0.1 fusion.14
  12.9 0.1 multiply_bitcast_fusion.3
  12.9 0.1 multiply_bitcast_fusion
  13.0 0.1 copy.16
  13.1 0.1 copy.13
  13.2 0.1 copy.14
  13.3 0.1 copy.15
  13.4 1.1 %add_divide_fusion.damp_any = f32[512,384]{1,0:T(8,128)} fusion(f32[384]{0:T(512)S(1)} %copy-done.6, f32[512]{0:T(512)S(1)} %multiply_add_fusion), kind=kLoop, calls=%fused_computation.35 | loop fusion | flops 393216 | bytes 790016 | tf_op jit(solution)/shard_map/div | solution.py:569
  14.5 0.1 maximum_maximum_fusion.weight_ref
  14.6 0.1 stack.38.place_ref
  14.6 2.2 %pair_lists.1 = (s32[1]{0:T(128)}, s32[257]{0:T(512)S(1)}, s32[257]{0:T(512)S(1)}) custom-call(s32[2,256]{1,0:T(2,128)S(1)} %bitcast.28, s32[256]{0:T(256)S(1)} %copy-done.2, s32[5]{0:T(128)S(1)} %stack.38.place_ref), custom_call_target="tpu_custom_call" | custom-call | bytes 8000000 | tf_op jit(solution)/shard_map/pair_lists/pallas_call | solution.py:170
  16.8 1.5 %reduce-precision_convert_fusion.1 = (bf16[4,384,256]{2,1,0:T(8,128)(2,1)S(1)}, bf16[4,384,256]{2,1,0:T(8,128)(2,1)S(1)}) fusion(f32[4]{0:T(128)S(1)} %compare_select_fusion.4, f32[384]{0:T(512)S(1)} %add_convert_fusion, s32[4]{0:T(128)S(1)} %iota_and_fusion, s32[256]{0:T(256)S(1)} %iota_multiply_fusion), kind=kLoop, calls=%fused_computation.8 | loop fusion | flops 11403264 | bytes 1575456 | tf_op jit(solution)/shard_map/convert_element_type | solution.py:58
  18.3 1.6 %pad_maximum_fusion.synth_any = bf16[4,384,768]{2,1,0:T(8,128)(2,1)} fusion(bf16[4,384,256]{2,1,0:T(8,128)(2,1)S(1)} %get-tuple-element.43, bf16[4,384,256]{2,1,0:T(8,128)(2,1)S(1)} %get-tuple-element.42), kind=kLoop, calls=%fused_computation.3 | loop fusion | flops 7077888 | bytes 3932160 | tf_op jit(solution)/shard_map/concatenate | solution.py:554
  19.9 1.6 %fusion.12 = (bf16[768,768]{1,0:T(8,128)(2,1)}, bf16[768,768]{1,0:T(8,128)(2,1)}) fusion(bf16[384,384]{1,0:T(8,128)(2,1)S(1)} %get-tuple-element.33, bf16[384,256]{1,0:T(8,128)(2,1)S(1)} %slice.81, bf16[384,128]{1,0:T(8,128)(2,1)S(1)} %slice.80, bf16[384,384]{1,0:T(8,128)(2,1)S(1)} %get-tuple-element.31, bf16[384,256]{1,0:T(8,128)(2,1)S(1)} %slice.83, ...), kind=kLoop, calls=%fused_computation.29 | loop fusion | flops 11206656 | bytes 3538944 | tf_op jit(solution)/shard_map/concatenate | solution.py:564
  21.5 1.6 %reduce-precision_convert_fusion = (bf16[4,256,384]{2,1,0:T(8,128)(2,1)S(1)}, bf16[4,256,384]{2,1,0:T(8,128)(2,1)S(1)}) fusion(f32[4]{0:T(128)S(1)} %compare_select_fusion.4, f32[384]{0:T(512)S(1)} %add_convert_fusion, s32[4]{0:T(128)S(1)} %iota_and_fusion, s32[256]{0:T(256)S(1)} %iota_multiply_fusion), kind=kLoop, calls=%fused_computation.6 | loop fusion | flops 11403264 | bytes 1575456 | tf_op jit(solution)/shard_map/convert_element_type | solution.py:58
  23.1 1.6 %pad_maximum_fusion.1.anal_any = bf16[4,256,1152]{2,1,0:T(8,128)(2,1)} fusion(bf16[4,256,384]{2,1,0:T(8,128)(2,1)S(1)} %get-tuple-element.41, bf16[4,256,384]{2,1,0:T(8,128)(2,1)S(1)} %get-tuple-element.40), kind=kLoop, calls=%fused_computation.4 | loop fusion | flops 7077888 | bytes 3932160 | tf_op jit(solution)/shard_map/concatenate | solution.py:556
  24.7 6.9 %all-to-all-done.moved_any = f32[16,64,384]{2,1,0:T(8,128)S(1)} async-done(((f32[16,64,384]{2,1,0:T(8,128)}), f32[16,64,384]{2,1,0:T(8,128)S(1)}, u32[]{:S(2)}, u32[]{:S(2)}) %all-to-all-start) | async-done | bytes 1572896 | tf_op jit(solution)/shard_map/all_to_all | solution.py:551
  31.6 15.0 %two_steps.1 = (f32[16,64,384]{2,1,0:T(8,128)}, f32[512,384]{1,0:T(8,128)}, f32[512,384]{1,0:T(8,128)}) custom-call(s32[1]{0:T(128)} %get-tuple-element.13.count_ref, s32[257]{0:T(512)S(1)} %get-tuple-element.14.spot_ref, s32[257]{0:T(512)S(1)} %get-tuple-element.15.mode_ref, f32[16,64,384]{2,1,0:T(8,128)S(1)} %all-to-all-done.moved_any, ...), custom_call_target="tpu_custom_call" | custom-call | flops 8000000000 | bytes 10000000 | tf_op jit(solution)/shard_map/two_steps/pallas_call | solution.py:367
  46.6 4.1 %collective-permute-start = (f32[512,384]{1,0:T(8,128)}, f32[512,384]{1,0:T(8,128)S(1)}, u32[]{:S(2)}, u32[]{:S(2)}) collective-permute-start(f32[512,384]{1,0:T(8,128)} %get-tuple-element.20), channel_id=1, source_target_pairs={{0,16},{16,0},{32,48},{48,32},{64,80},{80,64},{96,112},{112,96},{1... | collective-permute-start | bytes 2359304 | tf_op jit(solution)/shard_map/ppermute | solution.py:518
  50.7 3.8 %all-to-all-start.1 = ((f32[16,64,384]{2,1,0:T(8,128)}), f32[16,64,384]{2,1,0:T(8,128)S(1)}, u32[]{:S(2)}, u32[]{:S(2)}) async-start(f32[16,64,384]{2,1,0:T(8,128)} %get-tuple-element.17), calls=%async_computation.1 | async-start | bytes 3145728 | tf_op jit(solution)/shard_map/all_to_all | solution.py:582
  54.6 0.0 collective-permute-done
  54.6 0.0 copy-start
  54.6 0.1 slice_add_fusion.2
  54.7 1.7 %collective-permute-start.1 = (f32[128,384]{1,0:T(8,128)S(1)}, f32[128,384]{1,0:T(8,128)S(1)}, u32[]{:S(2)}, u32[]{:S(2)}) collective-permute-start(f32[128,384]{1,0:T(8,128)S(1)} %get-tuple-element.27), channel_id=1, source_target_pairs={{0,32},{16,48},{32,64},{48,80},{64,96},{80,112},{96,0},{112,16},{1... | collective-permute-start | bytes 589832 | tf_op jit(solution)/shard_map/ppermute | solution.py:525
  56.4 2.2 %collective-permute-start.3 = (f32[128,384]{1,0:T(8,128)S(1)}, f32[128,384]{1,0:T(8,128)S(1)}, u32[]{:S(2)}, u32[]{:S(2)}) collective-permute-start(f32[128,384]{1,0:T(8,128)S(1)} %get-tuple-element.28), channel_id=1, source_target_pairs={{0,96},{16,112},{32,0},{48,16},{64,32},{80,48},{96,64},{112,80},{1... | collective-permute-start | bytes 589832 | tf_op jit(solution)/shard_map/ppermute | solution.py:525
  58.6 1.2 %collective-permute-start.2 = (f32[128,384]{1,0:T(8,128)S(1)}, f32[128,384]{1,0:T(8,128)S(1)}, u32[]{:S(2)}, u32[]{:S(2)}) collective-permute-start(f32[128,384]{1,0:T(8,128)S(1)} %get-tuple-element.29), channel_id=1, source_target_pairs={{0,64},{16,80},{32,96},{48,112},{64,0},{80,16},{96,32},{112,48},{1... | collective-permute-start | bytes 589832 | tf_op jit(solution)/shard_map/ppermute | solution.py:525
  59.8 3.8 %collective-permute-done.1 = f32[128,384]{1,0:T(8,128)S(1)} collective-permute-done((f32[128,384]{1,0:T(8,128)S(1)}, f32[128,384]{1,0:T(8,128)S(1)}, u32[]{:S(2)}, u32[]{:S(2)}) %collective-permute-start.1) | collective-permute-done | bytes 196640 | tf_op jit(solution)/shard_map/ppermute | solution.py:525
  63.6 5.1 %collective-permute-done.2 = f32[128,384]{1,0:T(8,128)S(1)} collective-permute-done((f32[128,384]{1,0:T(8,128)S(1)}, f32[128,384]{1,0:T(8,128)S(1)}, u32[]{:S(2)}, u32[]{:S(2)}) %collective-permute-start.2) | collective-permute-done | bytes 196640 | tf_op jit(solution)/shard_map/ppermute | solution.py:525
  68.7 0.9 collective-permute-start.4
  69.7 1.8 %collective-permute-start.6 = (f32[32,384]{1,0:T(8,128)S(1)}, f32[32,384]{1,0:T(8,128)S(1)}, u32[]{:S(2)}, u32[]{:S(2)}) collective-permute-start(f32[32,384]{1,0:T(8,128)S(1)} %get-tuple-element.35), channel_id=1, source_target_pairs={{0,12},{1,13},{2,14},{3,15},{4,0},{5,1},{6,2},{7,3},{8,4},{9,5},{1... | collective-permute-start | bytes 147464 | tf_op jit(solution)/shard_map/ppermute | solution.py:525
  71.5 1.2 %collective-permute-start.5 = (f32[32,384]{1,0:T(8,128)S(1)}, f32[32,384]{1,0:T(8,128)S(1)}, u32[]{:S(2)}, u32[]{:S(2)}) collective-permute-start(f32[32,384]{1,0:T(8,128)S(1)} %get-tuple-element.36), channel_id=1, source_target_pairs={{0,8},{1,9},{2,10},{3,11},{4,12},{5,13},{6,14},{7,15},{8,0},{9,1},... | collective-permute-start | bytes 147464 | tf_op jit(solution)/shard_map/ppermute | solution.py:525
  72.7 4.9 %collective-permute-done.4 = f32[32,384]{1,0:T(8,128)S(1)} collective-permute-done((f32[32,384]{1,0:T(8,128)S(1)}, f32[32,384]{1,0:T(8,128)S(1)}, u32[]{:S(2)}, u32[]{:S(2)}) %collective-permute-start.4) | collective-permute-done | bytes 49184 | tf_op jit(solution)/shard_map/ppermute | solution.py:525
  77.7 1.1 %collective-permute-start.7 = (f32[8,384]{1,0:T(8,128)S(1)}, f32[8,384]{1,0:T(8,128)S(1)}, u32[]{:S(2)}, u32[]{:S(2)}) collective-permute-start(f32[8,384]{1,0:T(8,128)S(1)} %get-tuple-element.37), channel_id=1, source_target_pairs={{0,1},{1,2},{2,3},{3,0},{4,5},{5,6},{6,7},{7,4},{8,9},{9,10},{10,1... | collective-permute-start | bytes 36872 | tf_op jit(solution)/shard_map/ppermute | solution.py:525
  78.8 1.6 %collective-permute-start.9 = (f32[8,384]{1,0:T(8,128)S(1)}, f32[8,384]{1,0:T(8,128)S(1)}, u32[]{:S(2)}, u32[]{:S(2)}) collective-permute-start(f32[8,384]{1,0:T(8,128)S(1)} %get-tuple-element.38), channel_id=1, source_target_pairs={{0,3},{1,0},{2,1},{3,2},{4,7},{5,4},{6,5},{7,6},{8,11},{9,8},{10,9... | collective-permute-start | bytes 36872 | tf_op jit(solution)/shard_map/ppermute | solution.py:525
  80.4 0.7 collective-permute-start.8
  81.1 7.5 %retire_old.1.retired_ref = f32[8,2,384,384]{3,2,1,0:T(8,128)S(1)} custom-call(f32[8,2,384]{2,1,0:T(2,128)S(1)} %bitcast.26, f32[8,2,384,384]{3,2,1,0:T(8,128)} %bitcast.29), custom_call_target="tpu_custom_call" | custom-call | flops 300000000 | bytes 19000000 | tf_op jit(solution)/shard_map/retire_old/pallas_call | solution.py:430
  88.7 4.7 %admit_new.1 = (f32[8,2,384]{2,1,0:T(2,128)}, f32[8,2,384,384]{3,2,1,0:T(8,128)}) custom-call(f32[8,4]{1,0:T(8,128)S(1)} %maximum_maximum_fusion.weight_ref, f32[8,384]{1,0:T(8,128)S(1)} %fusion.22.snap_ref, f32[8,2,384]{2,1,0:T(2,128)S(1)} %bitcast.27, f32[8,2,384,384]{3,2,1,0:T(8,128)S(1)} %retire_old.1.retired_ref), custom_call_target="tpu_custom_call" | custom-call | flops 300000000 | bytes 10000000 | tf_op jit(solution)/shard_map/admit_new/pallas_call | solution.py:493
  93.4 1.3 %mode_major.1 = f32[2,32,16,384]{3,2,1,0:T(8,128)} custom-call(f32[16,64,384]{2,1,0:T(8,128)S(1)} %all-to-all-done.1.src), custom_call_target="tpu_custom_call" | custom-call | bytes 3145728 | tf_op jit(solution)/shard_map/mode_major/pallas_call | solution.py:129
  (32 shorter events, 0.2 us)
Async XLA Ops:
  3.1 7.8 %copy-start.4 = (f32[384,384]{1,0:T(8,128)S(1)}, f32[384,384]{1,0:T(8,128)}, u32[]{:S(2)}) copy-start(f32[384,384]{1,0:T(8,128)} %param.11) | copy-start | bytes 1769476
  3.1 28.5 %all-to-all-start = ((f32[16,64,384]{2,1,0:T(8,128)}), f32[16,64,384]{2,1,0:T(8,128)S(1)}, u32[]{:S(2)}, u32[]{:S(2)}) async-start(f32[16,64,384]{2,1,0:T(8,128)} %axial_major.1), calls=%async_computation | async-start | bytes 3145728 | tf_op jit(solution)/shard_map/all_to_all | solution.py:551
  10.8 1.1 %copy-start.5 = (f32[384,384]{1,0:T(8,128)S(1)}, f32[384,384]{1,0:T(8,128)}, u32[]{:S(2)}) copy-start(f32[384,384]{1,0:T(8,128)} %param.12) | copy-start | bytes 1769476
  10.9 1.9 %copy-start.7 = (s32[4]{0:T(128)S(1)}, s32[4]{0:T(128)}, u32[]{:S(2)}) copy-start(s32[4]{0:T(128)} %param.16) | copy-start | bytes 52
  10.9 2.4 %copy-start.6 = (f32[384]{0:T(512)S(1)}, f32[384]{0:T(512)}, u32[]{:S(2)}) copy-start(f32[384]{0:T(512)} %param.13) | copy-start | bytes 4612
  11.0 3.6 %copy-start.1 = (s32[256,2]{0,1:T(2,128)S(1)}, s32[256,2]{0,1:T(2,128)}, u32[]{:S(2)}) copy-start(s32[256,2]{0,1:T(2,128)} %param.14) | copy-start | bytes 6148
  11.1 3.6 %copy-start.2 = (s32[256]{0:T(256)S(1)}, s32[256]{0:T(256)}, u32[]{:S(2)}) copy-start(s32[256]{0:T(256)} %owner_ref.1) | copy-start | bytes 3076
  46.6 8.0 %collective-permute-start = (f32[512,384]{1,0:T(8,128)}, f32[512,384]{1,0:T(8,128)S(1)}, u32[]{:S(2)}, u32[]{:S(2)}) collective-permute-start(f32[512,384]{1,0:T(8,128)} %get-tuple-element.20), channel_id=1, source_target_pairs={{0,16},{16,0},{32,48},{48,32},{64,80},{80,64},{96,112},{112,96},{1... | collective-permute-start | bytes 2359304 | tf_op jit(solution)/shard_map/ppermute | solution.py:518
  50.7 3.9 %copy-start.3 = (f32[512,384]{1,0:T(8,128)S(1)}, f32[512,384]{1,0:T(8,128)}, u32[]{:S(2)}) copy-start(f32[512,384]{1,0:T(8,128)} %get-tuple-element.19) | copy-start | bytes 2359300
  50.7 42.7 %all-to-all-start.1 = ((f32[16,64,384]{2,1,0:T(8,128)}), f32[16,64,384]{2,1,0:T(8,128)S(1)}, u32[]{:S(2)}, u32[]{:S(2)}) async-start(f32[16,64,384]{2,1,0:T(8,128)} %get-tuple-element.17), calls=%async_computation.1 | async-start | bytes 3145728 | tf_op jit(solution)/shard_map/all_to_all | solution.py:582
  54.6 26.5 %copy-start = (f32[2,4,2,384]{3,2,1,0:T(2,128)S(1)}, f32[2,4,2,384]{3,2,1,0:T(2,128)}, u32[]{:S(2)}) copy-start(f32[2,4,2,384]{3,2,1,0:T(2,128)} %param.18) | copy-start | bytes 73732
  54.7 8.9 %collective-permute-start.1 = (f32[128,384]{1,0:T(8,128)S(1)}, f32[128,384]{1,0:T(8,128)S(1)}, u32[]{:S(2)}, u32[]{:S(2)}) collective-permute-start(f32[128,384]{1,0:T(8,128)S(1)} %get-tuple-element.27), channel_id=1, source_target_pairs={{0,32},{16,48},{32,64},{48,80},{64,96},{80,112},{96,0},{112,16},{1... | collective-permute-start | bytes 589832 | tf_op jit(solution)/shard_map/ppermute | solution.py:525
  56.4 7.2 %collective-permute-start.3 = (f32[128,384]{1,0:T(8,128)S(1)}, f32[128,384]{1,0:T(8,128)S(1)}, u32[]{:S(2)}, u32[]{:S(2)}) collective-permute-start(f32[128,384]{1,0:T(8,128)S(1)} %get-tuple-element.28), channel_id=1, source_target_pairs={{0,96},{16,112},{32,0},{48,16},{64,32},{80,48},{96,64},{112,80},{1... | collective-permute-start | bytes 589832 | tf_op jit(solution)/shard_map/ppermute | solution.py:525
  58.6 10.1 %collective-permute-start.2 = (f32[128,384]{1,0:T(8,128)S(1)}, f32[128,384]{1,0:T(8,128)S(1)}, u32[]{:S(2)}, u32[]{:S(2)}) collective-permute-start(f32[128,384]{1,0:T(8,128)S(1)} %get-tuple-element.29), channel_id=1, source_target_pairs={{0,64},{16,80},{32,96},{48,112},{64,0},{80,16},{96,32},{112,48},{1... | collective-permute-start | bytes 589832 | tf_op jit(solution)/shard_map/ppermute | solution.py:525
  68.7 8.9 %collective-permute-start.4 = (f32[32,384]{1,0:T(8,128)S(1)}, f32[32,384]{1,0:T(8,128)S(1)}, u32[]{:S(2)}, u32[]{:S(2)}) collective-permute-start(f32[32,384]{1,0:T(8,128)S(1)} %get-tuple-element.34), channel_id=1, source_target_pairs={{0,4},{1,5},{2,6},{3,7},{4,8},{5,9},{6,10},{7,11},{8,12},{9,13},{1... | collective-permute-start | bytes 147464 | tf_op jit(solution)/shard_map/ppermute | solution.py:525
  69.7 7.9 %collective-permute-start.6 = (f32[32,384]{1,0:T(8,128)S(1)}, f32[32,384]{1,0:T(8,128)S(1)}, u32[]{:S(2)}, u32[]{:S(2)}) collective-permute-start(f32[32,384]{1,0:T(8,128)S(1)} %get-tuple-element.35), channel_id=1, source_target_pairs={{0,12},{1,13},{2,14},{3,15},{4,0},{5,1},{6,2},{7,3},{8,4},{9,5},{1... | collective-permute-start | bytes 147464 | tf_op jit(solution)/shard_map/ppermute | solution.py:525
  71.5 6.1 %collective-permute-start.5 = (f32[32,384]{1,0:T(8,128)S(1)}, f32[32,384]{1,0:T(8,128)S(1)}, u32[]{:S(2)}, u32[]{:S(2)}) collective-permute-start(f32[32,384]{1,0:T(8,128)S(1)} %get-tuple-element.36), channel_id=1, source_target_pairs={{0,8},{1,9},{2,10},{3,11},{4,12},{5,13},{6,14},{7,15},{8,0},{9,1},... | collective-permute-start | bytes 147464 | tf_op jit(solution)/shard_map/ppermute | solution.py:525
  77.7 11.0 %collective-permute-start.7 = (f32[8,384]{1,0:T(8,128)S(1)}, f32[8,384]{1,0:T(8,128)S(1)}, u32[]{:S(2)}, u32[]{:S(2)}) collective-permute-start(f32[8,384]{1,0:T(8,128)S(1)} %get-tuple-element.37), channel_id=1, source_target_pairs={{0,1},{1,2},{2,3},{3,0},{4,5},{5,6},{6,7},{7,4},{8,9},{9,10},{10,1... | collective-permute-start | bytes 36872 | tf_op jit(solution)/shard_map/ppermute | solution.py:525
  78.8 9.9 %collective-permute-start.9 = (f32[8,384]{1,0:T(8,128)S(1)}, f32[8,384]{1,0:T(8,128)S(1)}, u32[]{:S(2)}, u32[]{:S(2)}) collective-permute-start(f32[8,384]{1,0:T(8,128)S(1)} %get-tuple-element.38), channel_id=1, source_target_pairs={{0,3},{1,0},{2,1},{3,2},{4,7},{5,4},{6,5},{7,6},{8,11},{9,8},{10,9... | collective-permute-start | bytes 36872 | tf_op jit(solution)/shard_map/ppermute | solution.py:525
  80.4 8.2 %collective-permute-start.8 = (f32[8,384]{1,0:T(8,128)S(1)}, f32[8,384]{1,0:T(8,128)S(1)}, u32[]{:S(2)}, u32[]{:S(2)}) collective-permute-start(f32[8,384]{1,0:T(8,128)S(1)} %get-tuple-element.39), channel_id=1, source_target_pairs={{0,2},{1,3},{2,0},{3,1},{4,6},{5,7},{6,4},{7,5},{8,10},{9,11},{10,... | collective-permute-start | bytes 36872 | tf_op jit(solution)/shard_map/ppermute | solution.py:525
